TPU v7x, 32 devices: a whole 2x2x4 slice. The times are simulated.
32 devices in a mesh: section: 2 (over core), expert: 8 (over z, x), dp: 2 (over y).
Axes of the slice: x: 2, y: 2, z: 4, core: 2. Of those that a mesh axis runs over, the one named last changes fastest.
Arguments:
- tokens: bfloat16 [2, 16, 65, 768], P(None, ('expert', 'dp')), may hold values from -6 to 6
- cotangent: bfloat16 [2, 16, 65, 768], P(None, ('expert', 'dp')), may hold values from -6 to 6
- routes: int32 [2, 2, 16, 65, 2], P('section', None, ('expert', 'dp')), may hold values from 0 to 7, all different within a row; in each aligned block of 65 rows (0 to 64, 65 to 129, ..., all dimensions but the last counted through in order) at most 25 rows name the same one
- norm1_gain: bfloat16 [2, 768], P('section', 'dp'), may hold values from 0.099609375 to 1.8984375
- qkv_weight: bfloat16 [2, 768, 2304], P('section', 'dp'), may hold values from -1 to 1
- out_weight: bfloat16 [2, 768, 768], P('section', 'dp'), may hold values from -1.25 to 1.25
- norm2_gain: bfloat16 [2, 768], P('section', 'dp'), may hold values from 0.099609375 to 1.8984375
- router_weight: bfloat16 [2, 768, 8], P('section', 'dp'), may hold values from -1 to 1
- expert_in: bfloat16 [2, 8, 768, 3072], P('section', 'expert', None, 'dp'), may hold values from -0.21875 to 0.21875
- expert_out: bfloat16 [2, 8, 3072, 768], P('section', 'expert', 'dp'), may hold values from -0.875 to 0.875
Outputs:
- boundary: float32 [2, 2, 16, 65, 768], P('section', None, ('expert', 'dp'))
- grad_norm1: float32 [2, 768], P('section', 'dp')
- grad_qkv: float32 [2, 768, 2304], P('section', 'dp')
- grad_proj: float32 [2, 768, 768], P('section', 'dp')
- grad_norm2: float32 [2, 768], P('section', 'dp')
- grad_router: float32 [2, 768, 8], P('section', 'dp')
- grad_expert_in: float32 [2, 8, 768, 3072], P('section', 'expert', None, 'dp')
- grad_expert_out: float32 [2, 8, 3072, 768], P('section', 'expert', 'dp')
Inputs may be any that keep to these rules, and one draw needn't show every extreme that they name: `routes`: in every aligned block of 65 rows (the images of one device in one micro-batch of one section) no expert is named by more than 25 rows, a bound that some block reaches; the two experts of a token differ.
All inputs are finite; a program needn't handle non-finite values.
Results may differ from a plain program's by a relative error of at most 0.03.
Values may be sent and summed in bfloat16 or wider, within the bound.
No kernel may reach another device: no remote copies, remote signals or barrier semaphores. Data moves between devices by JAX's collectives and lax.ppermute only.
A program may use at most 192 MiB of HBM per device.

v0:
```python
import jax
import jax.numpy as jnp
from jax import lax
from jax.sharding import PartitionSpec as P

HEAD = 64


EPSILON = 1e-06


def passed_along(value, axis, steps):
    count = lax.axis_size(axis)
    leading, last = (max(0, -steps), min(count, count - steps))
    return lax.ppermute(value, axis, [(source, source + steps) for source in range(leading, last)])


def shortened(x):
    return jax.tree.map(lambda a: a.astype(jnp.bfloat16) if a.dtype == jnp.float32 else a, x)


def norm_forward(values, norm_gain):
    center = values - jnp.mean(values, axis=-1, keepdims=True)
    inverse = lax.rsqrt(jnp.mean(center * center, axis=-1, keepdims=True) + EPSILON)
    normed = center * inverse
    return (normed * norm_gain, normed, inverse)


def norm_backward(grad_out, normed, inverse, norm_gain):
    grad_hat = grad_out * norm_gain
    grad_gain = jnp.sum(grad_out * normed, axis=0)
    grad_in = inverse * (
        grad_hat
        - jnp.mean(grad_hat, axis=-1, keepdims=True)
        - normed * jnp.mean(grad_hat * normed, axis=-1, keepdims=True)
    )
    return (grad_in, grad_gain)


def gelu_slope(pre_act):
    return (
        0.5 * (1.0 + lax.erf(pre_act * 0.7071067811865476))
        + pre_act * jnp.exp(-0.5 * pre_act * pre_act) * 0.3989422804014327
    )


def attention_forward(a_norm, weight_qkv, images):
    heads = weight_qkv.shape[1] // (3 * HEAD)
    qkv_rows = jnp.dot(a_norm, weight_qkv, preferred_element_type=jnp.float32).astype(jnp.bfloat16)
    shaped = qkv_rows.reshape(images, -1, 3, heads, HEAD)
    scores = jnp.einsum(
        "ishd,ithd->ihst", shaped[:, :, 0], shaped[:, :, 1], preferred_element_type=jnp.float32
    ) * HEAD ** (-0.5)
    row_max = jnp.max(scores, axis=-1, keepdims=True)
    log_total = row_max + jnp.log(jnp.sum(jnp.exp(scores - row_max), axis=-1, keepdims=True))
    attn_probs = jnp.exp(scores - log_total).astype(jnp.bfloat16)
    attended = jnp.einsum(
        "ihst,ithd->ishd", attn_probs, shaped[:, :, 2], preferred_element_type=jnp.float32
    )
    attended = attended.astype(jnp.bfloat16).reshape(a_norm.shape[0], heads * HEAD)
    return (qkv_rows, log_total, attended)


def attention_backward(grad_attended, qkv_rows, log_total, images):
    heads = qkv_rows.shape[1] // (3 * HEAD)
    shaped = qkv_rows.reshape(images, -1, 3, heads, HEAD)
    query_part = shaped[:, :, 0]
    key_part = shaped[:, :, 1]
    value_part = shaped[:, :, 2]
    score_scale = HEAD ** (-0.5)
    scores = (
        jnp.einsum("ishd,ithd->ihst", query_part, key_part, preferred_element_type=jnp.float32)
        * score_scale
    )
    attn_probs = jnp.exp(scores - log_total)
    probs_low = attn_probs.astype(jnp.bfloat16)
    grad_heads = grad_attended.reshape(images, -1, heads, HEAD)
    grad_value = jnp.einsum(
        "ihst,ishd->ithd", probs_low, grad_heads, preferred_element_type=jnp.float32
    )
    grad_probs = jnp.einsum(
        "ishd,ithd->ihst", grad_heads, value_part, preferred_element_type=jnp.float32
    )
    grad_scores = (
        attn_probs
        * (grad_probs - jnp.sum(attn_probs * grad_probs, axis=-1, keepdims=True))
        * score_scale
    )
    grad_scores = grad_scores.astype(jnp.bfloat16)
    grad_query = jnp.einsum(
        "ihst,ithd->ishd", grad_scores, key_part, preferred_element_type=jnp.float32
    )
    grad_key = jnp.einsum(
        "ihst,ishd->ithd", grad_scores, query_part, preferred_element_type=jnp.float32
    )
    stacked = jnp.stack([grad_query, grad_key, grad_value], axis=2)
    return stacked.astype(jnp.bfloat16).reshape(qkv_rows.shape[0], 3 * heads * HEAD)


def shards(
    tokens,
    cotangent,
    routes,
    norm1_gain,
    qkv_weight,
    out_weight,
    norm2_gain,
    router_weight,
    expert_in,
    expert_out,
):
    gathered = (
        lax.all_gather(norm1_gain, "dp", axis=1, tiled=True),
        lax.all_gather(qkv_weight, "dp", axis=1, tiled=True),
        lax.all_gather(out_weight, "dp", axis=1, tiled=True),
        lax.all_gather(norm2_gain, "dp", axis=1, tiled=True),
        lax.all_gather(router_weight, "dp", axis=1, tiled=True),
    )
    norm_one, weight_qkv, weight_proj, norm_two, weight_router = [member[0] for member in gathered]
    gain_one = norm_one.astype(jnp.float32)
    gain_two = norm_two.astype(jnp.float32)
    weight_in = expert_in[0, 0]
    weight_back = expert_out[0, 0]
    section_id = lax.axis_index("section")
    micro_count = tokens.shape[0]
    images = tokens.shape[1]
    seq_len = tokens.shape[2]
    model_width = tokens.shape[3]
    token_count = images * seq_len
    experts = weight_router.shape[1]
    capacity = max(2, (3 * token_count + experts - 1) // experts)
    pair_size = lax.axis_size("dp")
    section_routes = routes[0]

    def owner_trip(send_rows, work):
        spread = jnp.broadcast_to(
            send_rows.reshape(experts, 1, capacity, model_width),
            (experts, pair_size, capacity, model_width),
        )
        spread = spread.reshape(experts * pair_size, capacity, model_width)
        group_rows = lax.all_to_all(
            spread, ("expert", "dp"), split_axis=0, concat_axis=0, tiled=True
        )
        result, extra_out = work(group_rows)
        returned = lax.all_to_all(
            result.astype(jnp.bfloat16), ("expert", "dp"), split_axis=0, concat_axis=0, tiled=True
        ).astype(result.dtype)
        slot_total = jnp.sum(returned.reshape(experts, pair_size, capacity, model_width), axis=1)
        slot_total = slot_total.reshape(experts * capacity, model_width)
        return (slot_total, group_rows, extra_out)

    def expert_forward_work(group_rows):
        pre_act = jnp.einsum(
            "ksd,df->ksf", group_rows, weight_in, preferred_element_type=jnp.float32
        )
        hidden = jax.nn.gelu(pre_act, approximate=False).astype(jnp.bfloat16)
        return (
            jnp.einsum("ksf,fd->ksd", hidden, weight_back, preferred_element_type=jnp.float32),
            None,
        )

    def layer_backward(grad_in, kept_state):
        (
            a_norm,
            hat_one,
            inv_one,
            qkv_rows,
            log_total,
            attended,
            hat_two,
            inv_two,
            b_norm,
            router,
            pair_ids,
            gate_vals,
            slot_place,
            dispatch,
            group_rows,
            expert_rows,
        ) = kept_state
        grad_gate = jnp.sum(grad_in[:, None, :] * expert_rows.astype(jnp.float32), axis=-1)
        grad_rows = (
            (gate_vals[:, :, None] * grad_in[:, None, :])
            .astype(jnp.bfloat16)
            .reshape(-1, model_width)
        )
        send_grads = jnp.dot(dispatch, grad_rows, preferred_element_type=jnp.float32).astype(
            jnp.bfloat16
        )

        def expert_backward_work(group_grads):
            pre_act = jnp.einsum(
                "ksd,df->ksf", group_rows, weight_in, preferred_element_type=jnp.float32
            )
            hidden = jax.nn.gelu(pre_act, approximate=False).astype(jnp.bfloat16)
            grad_weight_back = jnp.einsum(
                "ksf,ksd->fd", hidden, group_grads, preferred_element_type=jnp.float32
            )
            grad_hidden = jnp.einsum(
                "ksd,fd->ksf", group_grads, weight_back, preferred_element_type=jnp.float32
            )
            grad_pre = (grad_hidden * gelu_slope(pre_act)).astype(jnp.bfloat16)
            grad_weight_in = jnp.einsum(
                "ksd,ksf->df", group_rows, grad_pre, preferred_element_type=jnp.float32
            )
            grad_slot_rows = jnp.einsum(
                "ksf,df->ksd", grad_pre, weight_in, preferred_element_type=jnp.float32
            )
            return (grad_slot_rows, (grad_weight_in, grad_weight_back))

        grad_total, unused, expert_terms = owner_trip(send_grads, expert_backward_work)
        grad_b_expert = jnp.sum(
            jnp.take(grad_total, slot_place, axis=0).reshape(token_count, 2, model_width), axis=1
        )
        choose = (
            pair_ids[:, :, None] == jnp.arange(experts, dtype=jnp.int32)[None, None, :]
        ).astype(jnp.float32)
        grad_prob = jnp.sum(choose * grad_gate[:, :, None], axis=1)
        grad_logit = router * (grad_prob - jnp.sum(router * grad_prob, axis=-1, keepdims=True))
        grad_logit = grad_logit.astype(jnp.bfloat16)
        grad_router_w = jnp.dot(b_norm.T, grad_logit, preferred_element_type=jnp.float32)
        grad_b = (
            jnp.dot(grad_logit, weight_router.T, preferred_element_type=jnp.float32) + grad_b_expert
        )
        grad_resid_norm, grad_gain_two = norm_backward(grad_b, hat_two, inv_two, gain_two)
        grad_resid = grad_in + grad_resid_norm
        grad_low = grad_resid.astype(jnp.bfloat16)
        grad_proj_w = jnp.dot(attended.T, grad_low, preferred_element_type=jnp.float32)
        grad_attended = jnp.dot(grad_low, weight_proj.T, preferred_element_type=jnp.float32).astype(
            jnp.bfloat16
        )
        grad_qkv_rows = attention_backward(grad_attended, qkv_rows, log_total, images)
        grad_qkv_w = jnp.dot(a_norm.T, grad_qkv_rows, preferred_element_type=jnp.float32)
        grad_a = jnp.dot(grad_qkv_rows, weight_qkv.T, preferred_element_type=jnp.float32)
        grad_token_norm, grad_gain_one = norm_backward(grad_a, hat_one, inv_one, gain_one)
        grad_tokens = grad_resid + grad_token_norm
        dense_terms = (grad_gain_one, grad_qkv_w, grad_proj_w, grad_gain_two, grad_router_w)
        return (grad_tokens, dense_terms, expert_terms)

    zero_rows = jnp.zeros((images, seq_len, model_width), jnp.bfloat16)
    forward_state = []
    forward_out = []
    passed = zero_rows
    for tick_index in range(micro_count + 1):
        if tick_index > 0:
            passed = passed_along(section_output, "section", 1)
        layer_in = jnp.where(section_id == 0, tokens[min(tick_index, micro_count - 1)], passed)
        micro_id = jnp.clip(tick_index - section_id, 0, micro_count - 1)
        route_ids = lax.dynamic_index_in_dim(section_routes, micro_id, 0, keepdims=False)
        token_rows = layer_in.reshape(token_count, model_width).astype(jnp.float32)
        a_full, layer_hat_one, layer_inv_one = norm_forward(token_rows, gain_one)
        layer_a_norm = a_full.astype(jnp.bfloat16)
        layer_qkv_rows, layer_log_total, layer_attended = attention_forward(
            layer_a_norm, weight_qkv, images
        )
        residual = token_rows + jnp.dot(
            layer_attended, weight_proj, preferred_element_type=jnp.float32
        )
        b_full, layer_hat_two, layer_inv_two = norm_forward(residual, gain_two)
        layer_b_norm = b_full.astype(jnp.bfloat16)
        logits = jnp.dot(layer_b_norm, weight_router, preferred_element_type=jnp.float32)
        layer_router = jax.nn.softmax(logits, axis=-1)
        layer_pair_ids = route_ids.reshape(token_count, 2)
        layer_gate_vals = jnp.take_along_axis(layer_router, layer_pair_ids, axis=1)
        flat_routes = route_ids.reshape(-1)
        onehot = (flat_routes[:, None] == jnp.arange(experts, dtype=jnp.int32)[None, :]).astype(
            jnp.int32
        )
        slot_pos = jnp.sum(onehot * (jnp.cumsum(onehot, axis=0) - 1), axis=1)
        slot_slot_place = flat_routes * capacity + slot_pos
        slot_dispatch = (
            slot_slot_place[None, :] == jnp.arange(experts * capacity, dtype=jnp.int32)[:, None]
        ).astype(jnp.bfloat16)
        layer_send_rows = jnp.dot(
            slot_dispatch, jnp.repeat(layer_b_norm, 2, axis=0), preferred_element_type=jnp.float32
        ).astype(jnp.bfloat16)
        layer_slot_total, layer_group_rows, layer_unused = owner_trip(
            layer_send_rows, expert_forward_work
        )
        slot_out = layer_slot_total.astype(jnp.bfloat16)
        layer_expert_rows = jnp.take(slot_out, slot_slot_place, axis=0).reshape(
            token_count, 2, model_width
        )
        layer_out = residual + jnp.sum(
            layer_gate_vals[:, :, None] * layer_expert_rows.astype(jnp.float32), axis=1
        )
        layer_kept_state = (
            layer_a_norm,
            layer_hat_one,
            layer_inv_one,
            layer_qkv_rows,
            layer_log_total,
            layer_attended,
            layer_hat_two,
            layer_inv_two,
            layer_b_norm,
            layer_router,
            layer_pair_ids,
            layer_gate_vals,
            slot_slot_place,
            slot_dispatch,
            layer_group_rows,
            layer_expert_rows,
        )
        layer_out, kept_state = (layer_out, layer_kept_state)
        section_output = layer_out.astype(jnp.bfloat16).reshape(images, seq_len, model_width)
        forward_state.append(kept_state)
        forward_out.append(layer_out)
    dense_sum = None
    expert_sum = None
    grad_inputs = []
    grad_carry = zero_rows
    for tick_index in range(micro_count + 1):
        kept_state = forward_state[micro_count - tick_index]
        own_cot = cotangent[micro_count - 1 - tick_index] if tick_index < micro_count else zero_rows
        passed_grad = passed_along(grad_carry, "section", -1) if tick_index > 0 else zero_rows
        grad_in = (
            jnp.where(section_id == 1, own_cot, passed_grad)
            .reshape(token_count, model_width)
            .astype(jnp.float32)
        )
        grad_tokens, dense_terms, expert_terms = layer_backward(grad_in, kept_state)
        grad_carry = grad_tokens.astype(jnp.bfloat16).reshape(images, seq_len, model_width)
        grad_inputs.append(grad_tokens)
        if dense_sum is None:
            dense_sum = dense_terms
            expert_sum = expert_terms
        else:
            dense_sum = tuple(
                (
                    first_term + second_term
                    for first_term, second_term in zip(dense_sum, dense_terms)
                )
            )
            expert_sum = tuple(
                (
                    first_term + second_term
                    for first_term, second_term in zip(expert_sum, expert_terms)
                )
            )
    end_values = []
    for micro_index in range(micro_count):
        picked = jnp.where(
            section_id == 0, grad_inputs[micro_count - micro_index], forward_out[micro_index + 1]
        )
        end_values.append(picked.reshape(images, seq_len, model_width))
    boundary = jnp.stack(end_values)[None]
    shares = jax.tree.map(
        lambda part: part.astype(jnp.float32),
        lax.psum_scatter(shortened(dense_sum), "dp", scatter_dimension=0, tiled=True),
    )
    full_sums = jax.tree.map(
        lambda part: part.astype(jnp.float32), lax.psum(shortened(shares), "expert")
    )
    return (
        boundary,
        full_sums[0][None],
        full_sums[1][None],
        full_sums[2][None],
        full_sums[3][None],
        full_sums[4][None],
        expert_sum[0][None, None],
        expert_sum[1][None, None],
    )


def solution(mesh):
    in_specs = (
        P(None, ("expert", "dp"), None, None),
        P(None, ("expert", "dp"), None, None),
        P("section", None, ("expert", "dp"), None, None),
        P("section", "dp"),
        P("section", "dp", None),
        P("section", "dp", None),
        P("section", "dp"),
        P("section", "dp", None),
        P("section", "expert", None, "dp"),
        P("section", "expert", "dp", None),
    )
    out_specs = (
        P("section", None, ("expert", "dp"), None, None),
        P("section", "dp"),
        P("section", "dp", None),
        P("section", "dp", None),
        P("section", "dp"),
        P("section", "dp", None),
        P("section", "expert", None, "dp"),
        P("section", "expert", "dp", None),
    )
    return jax.shard_map(shards, mesh=mesh, in_specs=in_specs, out_specs=out_specs, check_vma=False)
```

profile of v0, /device:TPU:28, one launch (start us, length us, event | category | flops | bytes accessed | tf_op | source)
XLA Modules:
  0.0 874.4 jit_solution(11960009164507809311)
XLA Ops:
  8.7 4.5 all_gather.15
  13.2 4.5 all_gather.18
  22.4 36.5 %all-gather.3.cloned.1.call-done = bf16[1,768,2304]{2,1,0:T(8,128)(2,1)} async-done(((bf16[1,384,2304]{2,1,0:T(8,128)(2,1)}), bf16[1,768,2304]{2,1,0:T(8,128)(2,1)}) %all-gather.3.cloned.1.call-update) | async-done | bytes 3538960 | tf_op jit(solution)/shard_map/all_gather | solution.py:114
  65.5 17.8 %all-gather.5.cloned.1.call-done = bf16[1,768,768]{2,1,0:T(8,128)(2,1)} async-done(((bf16[1,384,768]{2,1,0:T(8,128)(2,1)}), bf16[1,768,768]{2,1,0:T(8,128)(2,1)}) %all-gather.5.cloned.1.call-update) | async-done | bytes 1179664 | tf_op jit(solution)/shard_map/all_gather | solution.py:115
  90.4 6.9 all-to-all-start
  100.0 14.8 %all-to-all-done = bf16[16,25,768]{2,1,0:T(8,128)(2,1)} async-done(((bf16[16,25,768]{2,1,0:T(8,128)(2,1)}), bf16[16,25,768]{2,1,0:T(8,128)(2,1)}, u32[]{:S(2)}, u32[]{:S(2)}) %all-to-all-start) | async-done | bytes 614432 | tf_op jit(solution)/shard_map/all_to_all | solution.py:141
  119.5 7.0 fusion.28
  130.0 7.2 all-to-all-start.1
  137.5 5.1 all_gather.19
  146.7 7.0 all-to-all-done.1
  165.9 3.6 fusion.20
  185.2 25.8 %all_to_all.60 = bf16[16,25,768]{2,1,0:T(8,128)(2,1)S(1)} all-to-all(bf16[16,25,768]{2,1,0:T(8,128)(2,1)S(1)} %bitcast.575), channel_id=1, replica_groups=mesh['section'=2,'expert'=8,'dp'=2] {'expert','dp'}, dimensions={0} | all-to-all | bytes 1228800 | tf_op jit(solution)/shard_map/all_to_all | solution.py:141
  214.7 7.0 fusion.31
  225.1 7.5 all-to-all-start.3
  241.8 7.1 all-to-all-done.3
  267.2 3.5 fusion.23
  286.4 25.9 %all_to_all.61 = bf16[16,25,768]{2,1,0:T(8,128)(2,1)S(1)} all-to-all(bf16[16,25,768]{2,1,0:T(8,128)(2,1)S(1)} %bitcast.576), channel_id=1, replica_groups=mesh['section'=2,'expert'=8,'dp'=2] {'expert','dp'}, dimensions={0} | all-to-all | bytes 1228800 | tf_op jit(solution)/shard_map/all_to_all | solution.py:141
  315.9 7.0 fusion.34
  326.4 7.7 all-to-all-start.5
  344.2 6.1 all-to-all-done.5
  374.2 24.2 %all_to_all.62 = bf16[16,25,768]{2,1,0:T(8,128)(2,1)S(1)} all-to-all(bf16[16,25,768]{2,1,0:T(8,128)(2,1)S(1)} %bitcast.577), channel_id=1, replica_groups=mesh['section'=2,'expert'=8,'dp'=2] {'expert','dp'}, dimensions={0} | all-to-all | bytes 1228800 | tf_op jit(solution)/shard_map/all_to_all | solution.py:141
  398.3 4.4 fusion.65
  406.2 7.2 all-to-all-start.7
  414.1 15.3 %all-to-all-done.7 = bf16[16,25,768]{2,1,0:T(8,128)(2,1)} async-done(((bf16[16,25,768]{2,1,0:T(8,128)(2,1)}), bf16[16,25,768]{2,1,0:T(8,128)(2,1)}, u32[]{:S(2)}, u32[]{:S(2)}) %all-to-all-start.7) | async-done | bytes 614432 | tf_op jit(solution)/shard_map/all_to_all | solution.py:145
  459.7 4.1 fusion.217
  477.7 25.8 %all_to_all.63 = bf16[16,25,768]{2,1,0:T(8,128)(2,1)S(1)} all-to-all(bf16[16,25,768]{2,1,0:T(8,128)(2,1)S(1)} %bitcast.578), channel_id=1, replica_groups=mesh['section'=2,'expert'=8,'dp'=2] {'expert','dp'}, dimensions={0} | all-to-all | bytes 1228800 | tf_op jit(solution)/shard_map/all_to_all | solution.py:141
  503.5 4.4 fusion.66
  509.4 24.0 %all_to_all.64 = bf16[16,25,768]{2,1,0:T(8,128)(2,1)S(1)} all-to-all(bf16[16,25,768]{2,1,0:T(8,128)(2,1)S(1)} %fusion.98), channel_id=1, replica_groups=mesh['section'=2,'expert'=8,'dp'=2] {'expert','dp'}, dimensions={0} | all-to-all | bytes 1228800 | tf_op jit(solution)/shard_map/all_to_all | solution.py:145
  568.8 4.1 fusion.210
  586.1 24.1 %all_to_all.65 = bf16[16,25,768]{2,1,0:T(8,128)(2,1)S(1)} all-to-all(bf16[16,25,768]{2,1,0:T(8,128)(2,1)S(1)} %bitcast.579), channel_id=1, replica_groups=mesh['section'=2,'expert'=8,'dp'=2] {'expert','dp'}, dimensions={0} | all-to-all | bytes 1228800 | tf_op jit(solution)/shard_map/all_to_all | solution.py:141
  610.3 4.4 fusion.67
  618.2 6.7 all-to-all-start.11
  629.9 11.7 %all-to-all-done.11 = bf16[16,25,768]{2,1,0:T(8,128)(2,1)S(1)} async-done(((bf16[16,25,768]{2,1,0:T(8,128)(2,1)}), bf16[16,25,768]{2,1,0:T(8,128)(2,1)S(1)}, u32[]{:S(2)}, u32[]{:S(2)}) %all-to-all-start.11) | async-done | bytes 614432 | tf_op jit(solution)/shard_map/all_to_all | solution.py:145
  659.8 3.2 add_convert_fusion.1
  663.2 5.3 fusion.320
  668.6 4.2 fusion.317
  674.9 8.4 add_convert_fusion
  686.3 5.2 fusion.337
  691.5 3.5 fusion.339
  695.0 3.6 fusion.338
  698.7 3.6 fusion.340
  704.2 8.2 fusion.4
  712.5 23.4 %reduce-scatter.6.cloned.1.call-done = bf16[384,2304]{1,0:T(8,128)(2,1)} async-done(((bf16[768,2304]{1,0:T(8,128)(2,1)}), bf16[384,2304]{1,0:T(8,128)(2,1)}) %reduce-scatter.6.cloned.1.call-update) | async-done | bytes 1769488 | tf_op jit(solution)/shard_map/reduce_scatter | solution.py:350
  736.0 8.2 fusion.3
  746.8 4.9 all-reduce.7
  757.5 19.6 %all-reduce.5 = (bf16[1,384]{1,0:T(2,128)(2,1)S(1)}, bf16[1,384]{1,0:T(2,128)(2,1)S(1)}, bf16[1,384,8]{1,2,0:T(8,128)(2,1)S(1)}) all-reduce(bf16[1,384]{1,0:T(2,128)(2,1)S(1)} %broadcast_in_dim.104, bf16[1,384]{1,0:T(2,128)(2,1)S(1)} %broadcast_in_dim.110, ...), channel_id=1, replica_groups=mesh['section'=2,'expert'=8,'dp'=2] {'expert'}, use_global_device_ids=true, to_apply=%region_73.77 | all-reduce | flops 3840 | bytes 15360 | tf_op jit(solution)/shard_map/psum | solution.py:353
  778.9 82.4 %all-reduce.10.cloned.1.call-done = (bf16[1,384,2304]{2,1,0:T(8,128)(2,1)}, bf16[1,384,768]{2,1,0:T(8,128)(2,1)}) async-done(((bf16[1,384,2304]{2,1,0:T(8,128)(2,1)}, bf16[1,384,768]{2,1,0:T(8,128)(2,1)}), (bf16[1,384,2304]{2,1,0:T(8,128)(2,1)}, bf16[1,384,768]{2,1,0:T(8,128)(2,1)})) %all-reduce.10.cloned.1.call-update) | async-done | bytes 2359312 | tf_op jit(solution)/shard_map/psum | solution.py:353
  863.6 3.5 broadcast_in_dim.107
  (588 shorter events, 297.0 us)
Async XLA Ops:
  7.2 107.6 %copy-start = (bf16[1,1,768,1536]{3,2,1,0:T(8,128)(2,1)S(1)}, bf16[1,1,768,1536]{3,2,1,0:T(8,128)(2,1)}, u32[]{:S(2)}) copy-start(bf16[1,1,768,1536]{3,2,1,0:T(8,128)(2,1)} %param.24) | copy-start | bytes 7077892
  7.2 51.7 %all-gather.3.cloned.1.call-start = ((), (), s32[]{:S(2)}) async-start(), calls=%async_computation.15 | async-start | bytes 5308416 | tf_op jit(solution)/shard_map/all_gather | solution.py:114
  7.9 75.4 %all-gather.5.cloned.1.call-start = ((), (), s32[]{:S(2)}) async-start(), calls=%async_computation.16 | async-start | bytes 1769472 | tf_op jit(solution)/shard_map/all_gather | solution.py:115
  19.0 43.8 %copy-start.100 = (s32[1,1,1,65,2]{3,4,2,1,0:T(2,128)}, s32[1,1,1,65,2]{3,4,2,1,0:T(2,128)S(1)}, u32[]{:S(2)}) copy-start(s32[1,1,1,65,2]{3,4,2,1,0:T(2,128)S(1)} %get-tuple-element.81) | copy-start | bytes 1564
  19.0 79.2 %copy-start.99 = (s32[1,1,1,65,2]{3,4,2,1,0:T(2,128)}, s32[1,1,1,65,2]{3,4,2,1,0:T(2,128)S(1)}, u32[]{:S(2)}) copy-start(s32[1,1,1,65,2]{3,4,2,1,0:T(2,128)S(1)} %get-tuple-element.105) | copy-start | bytes 1564
  19.0 127.0 %copy-start.98 = (s32[1,1,1,65,2]{3,4,2,1,0:T(2,128)}, s32[1,1,1,65,2]{3,4,2,1,0:T(2,128)S(1)}, u32[]{:S(2)}) copy-start(s32[1,1,1,65,2]{3,4,2,1,0:T(2,128)S(1)} %get-tuple-element.103) | copy-start | bytes 1564
  20.5 79.5 %copy-start.95 = (s32[130]{0:T(256)}, s32[130]{0:T(256)S(1)}, u32[]{:S(2)}) copy-start(s32[130]{0:T(256)S(1)} %get-tuple-element.95) | copy-start | bytes 1564
  20.5 137.3 %copy-start.129 = (pred[130]{0:T(512)(128)(4,1)}, pred[130]{0:T(512)(128)(4,1)S(1)}, u32[]{:S(2)}) copy-start(pred[130]{0:T(512)(128)(4,1)S(1)} %get-tuple-element.94) | copy-start | bytes 394
  22.0 142.5 %copy-start.40 = (bf16[1,1,65,768]{3,0,2,1:T(2,128)(2,1)}, bf16[1,1,65,768]{3,0,2,1:T(2,128)(2,1)S(1)}, u32[]{:S(2)}) copy-start(bf16[1,1,65,768]{3,0,2,1:T(2,128)(2,1)S(1)} %get-tuple-element.100) | copy-start | bytes 299524
  22.1 61.2 %copy-start.18 = (bf16[1,1,65,768]{3,2,1,0:T(8,128)(2,1)}, bf16[1,1,65,768]{3,2,1,0:T(8,128)(2,1)S(1)}, u32[]{:S(2)}) copy-start(bf16[1,1,65,768]{3,2,1,0:T(8,128)(2,1)S(1)} %get-tuple-element.97) | copy-start | bytes 299524
  22.1 42.2 %copy-start.104 = (f32[65]{0:T(128)}, f32[65]{0:T(128)S(1)}, u32[]{:S(2)}) copy-start(f32[65]{0:T(128)S(1)} %broadcast_multiply_fusion.17) | copy-start | bytes 784
  22.3 43.2 %copy-start.121 = (f32[65]{0:T(128)}, f32[65]{0:T(128)S(1)}, u32[]{:S(2)}) copy-start(f32[65]{0:T(128)S(1)} %add_rsqrt_fusion.5) | copy-start | bytes 784
  22.4 153.6 %copy-start.68 = (f32[768]{0:T(1024)}, f32[768]{0:T(1024)S(1)}, u32[]{:S(2)}) copy-start(f32[768]{0:T(1024)S(1)} %convert_reduce_fusion.6) | copy-start | bytes 9220
  64.2 19.1 %copy-start.9 = (f32[12,65,65]{1,2,0:T(8,128)}, f32[12,65,65]{1,2,0:T(8,128)S(1)}, u32[]{:S(2)}) copy-start(f32[12,65,65]{1,2,0:T(8,128)S(1)} %get-tuple-element.111) | copy-start | bytes 608404
  64.3 26.1 %copy-start.76 = (f32[12,65]{1,0:T(8,128)}, f32[12,65]{1,0:T(8,128)S(1)}, u32[]{:S(2)}) copy-start(f32[12,65]{1,0:T(8,128)S(1)} %log_add_fusion.2) | copy-start | bytes 9364
  65.5 24.9 %copy-start.42 = (bf16[12,64,65]{2,1,0:T(8,128)(2,1)}, bf16[12,64,65]{2,1,0:T(8,128)(2,1)S(1)}, u32[]{:S(2)}) copy-start(bf16[12,64,65]{2,1,0:T(8,128)(2,1)S(1)} %convolution_convert_fusion.17) | copy-start | bytes 299524
  85.0 77.2 %copy-start.8 = (f32[65,768]{1,0:T(8,128)}, f32[65,768]{1,0:T(8,128)S(1)}, u32[]{:S(2)}) copy-start(f32[65,768]{1,0:T(8,128)S(1)} %get-tuple-element.113) | copy-start | bytes 599044
  85.0 13.2 %copy-start.119 = (f32[65]{0:T(128)}, f32[65]{0:T(128)S(1)}, u32[]{:S(2)}) copy-start(f32[65]{0:T(128)S(1)} %broadcast_multiply_fusion.16) | copy-start | bytes 784
  85.2 12.7 %copy-start.130 = (f32[65]{0:T(128)}, f32[65]{0:T(128)S(1)}, u32[]{:S(2)}) copy-start(f32[65]{0:T(128)S(1)} %add_rsqrt_fusion.4) | copy-start | bytes 784
  85.4 58.0 %copy-start.43 = (bf16[65,768]{1,0:T(8,128)(2,1)}, bf16[65,768]{1,0:T(8,128)(2,1)S(1)}, u32[]{:S(2)}) copy-start(bf16[65,768]{1,0:T(8,128)(2,1)S(1)} %multiply_convert_fusion.5) | copy-start | bytes 299524
  90.4 24.3 %all-to-all-start = ((bf16[16,25,768]{2,1,0:T(8,128)(2,1)}), bf16[16,25,768]{2,1,0:T(8,128)(2,1)}, u32[]{:S(2)}, u32[]{:S(2)}) async-start(bf16[16,25,768]{2,1,0:T(8,128)(2,1)} %bitcast.574), calls=%async_computation | async-start | bytes 1572864 | tf_op jit(solution)/shard_map/all_to_all | solution.py:141
  130.0 23.7 %all-to-all-start.1 = ((bf16[16,25,768]{2,1,0:T(8,128)(2,1)}), bf16[16,25,768]{2,1,0:T(8,128)(2,1)}, u32[]{:S(2)}, u32[]{:S(2)}) async-start(bf16[16,25,768]{2,1,0:T(8,128)(2,1)} %fusion.104), calls=%async_computation.1 | async-start | bytes 1572864 | tf_op jit(solution)/shard_map/all_to_all | solution.py:145
  137.2 19.7 %copy-start.113 = (s32[1024]{0:T(1024)}, s32[1024]{0:T(1024)S(1)}, u32[]{:S(2)}) copy-start(s32[1024]{0:T(1024)S(1)} %pad_clamp_fusion.2) | copy-start | bytes 12292
  146.7 16.9 %copy-start.131 = (s32[130]{0:T(256)S(1)}, s32[130]{0:T(256)}, u32[]{:S(2)}) copy-start(s32[130]{0:T(256)} %fusion.292) | copy-start | bytes 1564
  146.7 16.9 %copy-start.132 = (s32[130]{0:T(256)S(1)}, s32[130]{0:T(256)}, u32[]{:S(2)}) copy-start(s32[130]{0:T(256)} %fusion.294) | copy-start | bytes 1564
  162.3 2.2 collective-permute-start
  164.2 70.1 %copy-start.96 = (s32[130]{0:T(256)}, s32[130]{0:T(256)S(1)}, u32[]{:S(2)}) copy-start(s32[130]{0:T(256)S(1)} %get-tuple-element.138) | copy-start | bytes 1564
  225.1 23.8 %all-to-all-start.3 = ((bf16[16,25,768]{2,1,0:T(8,128)(2,1)}), bf16[16,25,768]{2,1,0:T(8,128)(2,1)}, u32[]{:S(2)}, u32[]{:S(2)}) async-start(bf16[16,25,768]{2,1,0:T(8,128)(2,1)} %fusion.107), calls=%async_computation.3 | async-start | bytes 1572864 | tf_op jit(solution)/shard_map/all_to_all | solution.py:145
  238.9 16.8 %copy-start.128 = (pred[130]{0:T(512)(128)(4,1)S(1)}, pred[130]{0:T(512)(128)(4,1)}, u32[]{:S(2)}) copy-start(pred[130]{0:T(512)(128)(4,1)} %get-tuple-element.137) | copy-start | bytes 394
  262.6 2.2 collective-permute-start.1
  270.7 10.9 %copy-start.97 = (s32[130]{0:T(256)S(1)}, s32[130]{0:T(256)}, u32[]{:S(2)}) copy-start(s32[130]{0:T(256)} %get-tuple-element.79) | copy-start | bytes 1564
  277.0 37.3 %copy-start.117 = (f32[65]{0:T(128)}, f32[65]{0:T(128)S(1)}, u32[]{:S(2)}) copy-start(f32[65]{0:T(128)S(1)} %broadcast_multiply_fusion.12) | copy-start | bytes 784
  324.1 10.0 %copy-start.133 = (s32[65,2,1]{0,1,2:T(2,128)S(1)}, s32[65,2,1]{0,1,2:T(2,128)}, u32[]{:S(2)}) copy-start(s32[65,2,1]{0,1,2:T(2,128)} %get-tuple-element.80) | copy-start | bytes 1564
  326.4 23.9 %all-to-all-start.5 = ((bf16[16,25,768]{2,1,0:T(8,128)(2,1)}), bf16[16,25,768]{2,1,0:T(8,128)(2,1)}, u32[]{:S(2)}, u32[]{:S(2)}) async-start(bf16[16,25,768]{2,1,0:T(8,128)(2,1)} %fusion.110), calls=%async_computation.5 | async-start | bytes 1572864 | tf_op jit(solution)/shard_map/all_to_all | solution.py:145
  338.5 23.3 %copy-start.101 = (s32[1,1,1,65,2]{3,4,2,1,0:T(2,128)S(1)}, s32[1,1,1,65,2]{3,4,2,1,0:T(2,128)}, u32[]{:S(2)}) copy-start(s32[1,1,1,65,2]{3,4,2,1,0:T(2,128)} %copy-done.100) | copy-start | bytes 1564
  406.2 23.1 %all-to-all-start.7 = ((bf16[16,25,768]{2,1,0:T(8,128)(2,1)}), bf16[16,25,768]{2,1,0:T(8,128)(2,1)}, u32[]{:S(2)}, u32[]{:S(2)}) async-start(bf16[16,25,768]{2,1,0:T(8,128)(2,1)} %fusion.95), calls=%async_computation.7 | async-start | bytes 1572864 | tf_op jit(solution)/shard_map/all_to_all | solution.py:145
  446.3 13.4 %copy-start.88 = (f32[65]{0:T(128)S(1)}, f32[65]{0:T(128)}, u32[]{:S(2)}) copy-start(f32[65]{0:T(128)} %copy-done.87) | copy-start | bytes 784
  464.6 3.5 collective-permute-start.2
  534.4 11.2 %copy-start.75 = (f32[65,8]{0,1:T(8,128)S(1)}, f32[65,8]{0,1:T(8,128)}, u32[]{:S(2)}) copy-start(f32[65,8]{0,1:T(8,128)} %copy-done.74) | copy-start | bytes 6244
  555.4 13.4 %copy-start.85 = (f32[65]{0:T(128)S(1)}, f32[65]{0:T(128)}, u32[]{:S(2)}) copy-start(f32[65]{0:T(128)} %copy-done.84) | copy-start | bytes 784
  573.8 3.5 collective-permute-start.3
  618.2 9.8 %copy-start.50 = (bf16[12,64,65]{2,1,0:T(8,128)(2,1)S(1)}, bf16[12,64,65]{2,1,0:T(8,128)(2,1)}, u32[]{:S(2)}) copy-start(bf16[12,64,65]{2,1,0:T(8,128)(2,1)} %copy-done.49) | copy-start | bytes 299524
  618.2 23.4 %all-to-all-start.11 = ((bf16[16,25,768]{2,1,0:T(8,128)(2,1)}), bf16[16,25,768]{2,1,0:T(8,128)(2,1)S(1)}, u32[]{:S(2)}, u32[]{:S(2)}) async-start(bf16[16,25,768]{2,1,0:T(8,128)(2,1)} %fusion.101), calls=%async_computation.11 | async-start | bytes 1572864 | tf_op jit(solution)/shard_map/all_to_all | solution.py:145
  624.9 87.6 %reduce-scatter.8.cloned.1.call-start = ((), (), s32[]{:S(2)}) async-start(), calls=%async_computation.18 | async-start | bytes 1769472 | tf_op jit(solution)/shard_map/reduce_scatter | solution.py:350
  643.6 16.3 %copy-start.4 = (f32[768,768]{1,0:T(8,128)S(1)}, f32[768,768]{1,0:T(8,128)}, u32[]{:S(2)}) copy-start(f32[768,768]{1,0:T(8,128)} %fusion.273) | copy-start | bytes 7077892
  663.1 72.7 %reduce-scatter.6.cloned.1.call-start = ((), (), s32[]{:S(2)}) async-start(), calls=%async_computation.17 | async-start | bytes 5308416 | tf_op jit(solution)/shard_map/reduce_scatter | solution.py:350
  683.4 73.2 %reduce-scatter.10.cloned.1.call-start = ((), (), s32[]{:S(2)}) async-start(), calls=%async_computation.19 | async-start | bytes 294912
  704.2 157.1 %all-reduce.10.cloned.1.call-start = ((), (), s32[]{:S(2)}) async-start(), calls=%async_computation.20 | async-start | bytes 4718592 | tf_op jit(solution)/shard_map/psum | solution.py:353
  (112 other events, 433.7 us)
Sparse Core Ops, SparseCore 0:
  9.5 49.3 all-gather.2
  60.5 22.7 all-gather.4
  663.2 22.1 reduce-scatter.7
  688.1 47.7 reduce-scatter.5
  737.9 11.0 reduce-scatter.9
  752.4 108.8 all-reduce.9
where the time goes:
time: 890 us; the launch traced here: 874 us
  waiting for transfers between devices  227 us (26%)
  blocking collectives  188 us (21%)
  matrix products  166 us (19%)
  local copies, waits for them, and re-layouts  131 us (15%)
  other arithmetic  95.5 us (11%)
  starting transfers between devices  49.1 us (6%)
  between operations  17.2 us (2%)
    all_to_all x5, blocking collectives, owner_trip(): lax.all_to_all(spread, ('expert', 'dp'), split_axis=0, concat_axis=0, til...  126 us
    psum x1, waiting for transfers between devices, shards(): lax.psum(shortened(shares), 'expert')  82.4 us
    all_to_all x5, waiting for transfers between devices, owner_trip(): lax.all_to_all(result.astype(jnp.bfloat16), ('expert', 'dp'), split_axis=...  47.1 us
    all_gather x1, waiting for transfers between devices, shards(): lax.all_gather(qkv_weight, 'dp', axis=1, tiled=True)  36.5 us
    all_to_all x5, starting transfers between devices, owner_trip(): lax.all_to_all(result.astype(jnp.bfloat16), ('expert', 'dp'), split_axis=...  36.4 us
    unnamed x294, local copies, waits for them, and re-layouts  26.3 us
    all_to_all x1, blocking collectives, owner_trip(): lax.all_to_all(result.astype(jnp.bfloat16), ('expert', 'dp'), split_axis=...  24 us
    reduce_scatter x2, waiting for transfers between devices, shards(): lax.psum_scatter(shortened(dense_sum), 'dp', scatter_dimension=0, tiled=T...  23.4 us
  transfers between devices with their start and end apart: 16, of which 14 were waited for; matrix products, arithmetic and copies ran while one was open for 12% of the time, Pallas kernels for 0%

commit v1 on v0

v1 whole, which is shorter than its diff:
```python
import functools

import jax
import jax.numpy as jnp
import numpy as np
from jax import lax
from jax.experimental import pallas as pl
from jax.experimental.pallas import tpu as pltpu
from jax.sharding import PartitionSpec as P

HEAD = 64
EPSILON = 1e-06
BF = jnp.bfloat16
F32 = jnp.float32
SCALE = HEAD ** (-0.5)


def dot(a, b):
    return jnp.dot(a, b, preferred_element_type=F32)


def dot_nt(a, b):
    return lax.dot_general(a, b, (((1,), (1,)), ((), ())), preferred_element_type=F32)


def dot_tn(a, b):
    return lax.dot_general(a, b, (((0,), (0,)), ((), ())), preferred_element_type=F32)


def row_mean(v):
    return jnp.mean(v, axis=-1, keepdims=True)


def norm_parts(values):
    center = values - row_mean(values)
    inverse = lax.rsqrt(row_mean(center * center) + EPSILON)
    return center * inverse, inverse


def norm_backward(grad_out, normed, inverse, gain):
    grad_hat = grad_out * gain
    return inverse * (grad_hat - row_mean(grad_hat) - normed * row_mean(grad_hat * normed))


def softmax_router(b_norm, router_rows):
    logits = dot_nt(b_norm, router_rows)
    e = jnp.exp(logits - jnp.max(logits, axis=-1, keepdims=True))
    return e / jnp.sum(e, axis=-1, keepdims=True)


def expert_choice(routes_col, j, experts):
    rows = routes_col.shape[0]
    ids = lax.broadcasted_iota(jnp.int32, (rows, experts), 1)
    return (routes_col[:, j : j + 1] == ids).astype(F32)


def slots_by_token(routes_col, sid_row):
    rows = routes_col.shape[0]
    want, place = sid_row[0:1, :], sid_row[1:2, :].astype(F32)
    m0 = (routes_col[:, 0:1] == want).astype(F32)
    m1 = (routes_col[:, 1:2] == want).astype(F32)
    r = lax.broadcasted_iota(jnp.int32, (rows, rows), 0)
    c = lax.broadcasted_iota(jnp.int32, (rows, rows), 1)
    before = (c < r).astype(F32).astype(BF)
    pos = dot(before, (m0 + m1).astype(BF))
    here = (pos == place).astype(F32)
    return (m0 * here).astype(BF), (m1 * here).astype(BF)


def slots_by_slot(routes_row, sid_col):
    rows = routes_row.shape[1]
    want, place = sid_col[:, 0:1], sid_col[:, 1:2].astype(F32)
    m0 = (routes_row[0:1, :] == want).astype(F32)
    m1 = (routes_row[1:2, :] == want).astype(F32)
    r = lax.broadcasted_iota(jnp.int32, (rows, rows), 0)
    c = lax.broadcasted_iota(jnp.int32, (rows, rows), 1)
    before = (r < c).astype(F32).astype(BF)
    pos = dot((m0 + m1).astype(BF), before)
    here = (pos == place).astype(F32)
    return (m0 * here).astype(BF), (m1 * here).astype(BF)


def pair_masks():
    lane = lax.broadcasted_iota(jnp.int32, (1, 2 * HEAD), 1)
    first = (lane < HEAD).astype(F32)
    return first.astype(BF), (1.0 - first).astype(BF), first


def pair_probs(q2, k2, ma, mb, tokens):
    qs = jnp.concatenate([q2 * ma, q2 * mb], axis=0)
    scores = dot_nt(qs, k2) * SCALE
    col = lax.broadcasted_iota(jnp.int32, scores.shape, 1)
    scores = jnp.where(col < tokens, scores, -1e30)
    e = jnp.exp(scores - jnp.max(scores, axis=-1, keepdims=True))
    return qs, e / jnp.sum(e, axis=-1, keepdims=True)


def weight_copies(sel, half, d, own, swapped, dst, sem, base):
    near = pl.multiple_of(d * half, half)
    far = pl.multiple_of((1 - d) * half, half)

    def copies(src):
        return (
            pltpu.make_async_copy(src[0], dst.at[pl.ds(near, half)], sem.at[base]),
            pltpu.make_async_copy(src[1], dst.at[pl.ds(far, half)], sem.at[base + 1]),
        )

    @pl.when(sel)
    def _():
        for copy in copies(own):
            copy.start()

    @pl.when(jnp.logical_not(sel))
    def _():
        for copy in copies(swapped):
            copy.start()

    def wait():
        for copy in copies(own):
            copy.wait()

    return wait


def forward_body(layer, tokens, experts, second, *refs):
    if second:
        (ids, ret_p, r_p, small_p, rc_p, cot, small, rc, rr, sid_row, sid_col) = refs[:11]
        refs = refs[11:]
    else:
        (ids, x_ref, small, rr, sid_col) = refs[:5]
        refs = refs[5:]
    weights, refs = refs[:8], refs[8:]
    if second:
        send, r_out, qkv_out, attn_out, a_out, x_out, wq, wp, sem = refs
    else:
        send, r_out, qkv_out, attn_out, a_out, wq, wp, sem = refs
    width = wq.shape[0]
    sel = ids[0] == layer
    d = ids[1]
    half = width // 2
    wait_q = weight_copies(sel, half, d, weights[0:2], weights[2:4], wq, sem, 0)
    wait_p = weight_copies(sel, half, d, weights[4:6], weights[6:8], wp, sem, 2)
    if second:
        rows, routes_p = r_p[...], rc_p[...]
        normed, _ = norm_parts(rows)
        b_prev = (normed * small_p[1:2, :].astype(F32)).astype(BF)
        router = softmax_router(b_prev, small_p[2:, :])
        d0, d1 = slots_by_token(routes_p, sid_row[...])
        total = rows
        for j, dj in ((0, d0), (1, d1)):
            gate = jnp.sum(router * expert_choice(routes_p, j, experts), axis=-1, keepdims=True)
            total = total + gate * dot(dj, ret_p[...]).astype(BF).astype(F32)
        x = total.astype(BF)
        x_out[...] = x
    else:
        x = x_ref[...]
    x = x.astype(F32)
    normed, _ = norm_parts(x)
    a_norm = (normed * small[0:1, :].astype(F32)).astype(BF)
    a_out[...] = a_norm
    wait_q()
    qkv_out[...] = dot(a_norm, wq[...]).astype(BF)
    ma, mb, first = pair_masks()
    rows = x.shape[0]
    for p in range(width // (2 * HEAD)):
        at = p * 2 * HEAD
        q2 = qkv_out[:, at : at + 2 * HEAD]
        k2 = qkv_out[:, width + at : width + at + 2 * HEAD]
        v2 = qkv_out[:, 2 * width + at : 2 * width + at + 2 * HEAD]
        _, probs = pair_probs(q2, k2, ma, mb, tokens)
        o = dot(probs.astype(BF), v2)
        attn_out[:, at : at + 2 * HEAD] = (o[:rows] * first + o[rows:] * (1.0 - first)).astype(BF)
    wait_p()
    r = x + dot(attn_out[...], wp[...])
    r_out[...] = r
    normed, _ = norm_parts(r)
    b_norm = (normed * small[1:2, :].astype(F32)).astype(BF)
    t0, t1 = slots_by_slot(rr[...], sid_col[...])
    send[:, 0:width] = dot(t0 + t1, b_norm).astype(BF)
    if second:
        router = softmax_router(b_norm, small[2:, :])
        routes = rc[...]
        send[:, width:] = scatter_grads(router, routes, cot[...].astype(F32), t0, t1, experts)


def scatter_grads(router, routes, grad, t0, t1, experts):
    total = None
    for j, tj in ((0, t0), (1, t1)):
        gate = jnp.sum(router * expert_choice(routes, j, experts), axis=-1, keepdims=True)
        part = dot(tj, (gate * grad).astype(BF))
        total = part if total is None else total + part
    return total.astype(BF)


def backward_body(layer, tokens, experts, last, *refs):
    if last:
        (ids, ret, dsl, grad, r_ref, x_ref, qkv, small, rc, sid_row) = refs[:10]
        refs = refs[10:]
    else:
        (ids, ret, grad, r_ref, x_ref, qkv, small, rc, sid_row) = refs[:9]
        (r_p, small_p, rc_p, rr_p, sid_col) = refs[9:14]
        refs = refs[14:]
    weights, refs = refs[:8], refs[8:]
    if last:
        dqkv_out, dr_out, sm_out, dh_out, wq, wp, sem = refs
    else:
        dqkv_out, dr_out, sm_out, out_ref, c_out, send, wq, wp, sem = refs
    width = wq.shape[0]
    sel = ids[0] == layer
    d = ids[1]
    half = width // 2
    wait_p = weight_copies(sel, half, d, weights[4:6], weights[6:8], wp, sem, 2)
    wait_q = weight_copies(sel, half, d, weights[0:2], weights[2:4], wq, sem, 0)
    c = grad[...].astype(F32)
    r = r_ref[...]
    hat2, inv2 = norm_parts(r)
    gain2 = small[1:2, :].astype(F32)
    b_norm = (hat2 * gain2).astype(BF)
    router = softmax_router(b_norm, small[2:, :])
    routes = rc[...]
    d0, d1 = slots_by_token(routes, sid_row[...])
    grad_prob = jnp.zeros(router.shape, F32)
    total = r
    for j, dj in ((0, d0), (1, d1)):
        choice = expert_choice(routes, j, experts)
        rows_j = dot(dj, ret[:, 0:width]).astype(BF).astype(F32)
        grad_prob = grad_prob + choice * jnp.sum(c * rows_j, axis=-1, keepdims=True)
        if not last:
            gate = jnp.sum(router * choice, axis=-1, keepdims=True)
            total = total + gate * rows_j
    if not last:
        out_ref[...] = total
    slot_grads = dsl[...] if last else ret[:, width:]
    grad_b = dot(d0 + d1, slot_grads)
    grad_logit = router * (grad_prob - jnp.sum(router * grad_prob, axis=-1, keepdims=True))
    grad_logit = grad_logit.astype(BF)
    sm_out[2:, :] = dot_tn(grad_logit, b_norm)
    grad_b = grad_b + dot(grad_logit, small[2:, :])
    sm_out[1:2, :] = jnp.sum(grad_b * hat2, axis=0, keepdims=True)
    grad_r = c + norm_backward(grad_b, hat2, inv2, gain2)
    grad_low = grad_r.astype(BF)
    dr_out[...] = grad_low
    wait_p()
    grad_attn = dot_nt(grad_low, wp[...]).astype(BF)
    ma, mb, first = pair_masks()
    rows = r.shape[0]
    for p in range(width // (2 * HEAD)):
        at = p * 2 * HEAD
        q2 = qkv[:, at : at + 2 * HEAD]
        k2 = qkv[:, width + at : width + at + 2 * HEAD]
        v2 = qkv[:, 2 * width + at : 2 * width + at + 2 * HEAD]
        g2 = grad_attn[:, at : at + 2 * HEAD]
        qs, probs = pair_probs(q2, k2, ma, mb, tokens)
        gs = jnp.concatenate([g2 * ma, g2 * mb], axis=0)
        grad_v = dot_tn(probs.astype(BF), gs)
        grad_p = dot_nt(gs, v2)
        grad_s = probs * (grad_p - jnp.sum(probs * grad_p, axis=-1, keepdims=True)) * SCALE
        grad_s = grad_s.astype(BF)
        gq = dot(grad_s, k2)
        grad_k = dot_tn(grad_s, qs)
        dqkv_out[:, at : at + 2 * HEAD] = (gq[:rows] * first + gq[rows:] * (1.0 - first)).astype(BF)
        dqkv_out[:, width + at : width + at + 2 * HEAD] = grad_k.astype(BF)
        dqkv_out[:, 2 * width + at : 2 * width + at + 2 * HEAD] = grad_v.astype(BF)
    wait_q()
    grad_a = dot_nt(dqkv_out[...], wq[...])
    hat1, inv1 = norm_parts(x_ref[...].astype(F32))
    sm_out[0:1, :] = jnp.sum(grad_a * hat1, axis=0, keepdims=True)
    grad_h = grad_r + norm_backward(grad_a, hat1, inv1, small[0:1, :].astype(F32))
    if last:
        dh_out[...] = grad_h
    else:
        c_low = grad_h.astype(BF)
        c_out[...] = c_low
        normed, _ = norm_parts(r_p[...])
        b_prev = (normed * small_p[1:2, :].astype(F32)).astype(BF)
        router_p = softmax_router(b_prev, small_p[2:, :])
        t0, t1 = slots_by_slot(rr_p[...], sid_col[...])
        send[...] = scatter_grads(router_p, rc_p[...], c_low.astype(F32), t0, t1, experts)


def chosen_copies(sel, own, swapped, dst, sem):
    def start(src):
        for i, (a, b) in enumerate(zip(src, dst)):
            pltpu.make_async_copy(a, b, sem.at[i]).start()

    @pl.when(sel)
    def _():
        start(own)

    @pl.when(jnp.logical_not(sel))
    def _():
        start(swapped)

    return [functools.partial(lambda a, b, i: pltpu.make_async_copy(a, b, sem.at[i]).wait(), a, b, i) for i, (a, b) in enumerate(zip(own, dst))]


FCHUNK = 256


def gelu_parts(pre):
    half_erf = 0.5 * (1.0 + lax.erf(pre * 0.7071067811865476))
    slope = half_erf + pre * jnp.exp(-0.5 * pre * pre) * 0.3989422804014327
    return pre * half_erf, slope


def expert_forward_body(layer, ids, g, own_in, own_out, sw_in, sw_out, res, hid, slope, win, wout, sem):
    waits = chosen_copies(ids[0] == layer, (own_in, own_out), (sw_in, sw_out), (win, wout), sem)
    waits[0]()
    for f in range(0, win.shape[1], FCHUNK):
        pre = dot(g[...], win[:, f : f + FCHUNK])
        act, grad = gelu_parts(pre)
        hid[:, f : f + FCHUNK] = act.astype(BF)
        slope[:, f : f + FCHUNK] = grad.astype(BF)
    waits[1]()
    res[...] = dot(hid[...], wout[...]).astype(BF)


def expert_both_body(layer, ids, g, own_in, own_out, sw_in, sw_out, res, hid, dpre, win, wout, sem):
    waits = chosen_copies(ids[0] == layer, (own_in, own_out), (sw_in, sw_out), (win, wout), sem)
    width = win.shape[0]
    waits[0]()
    waits[1]()
    for f in range(0, win.shape[1], FCHUNK):
        pre = dot(g[:, :width], win[:, f : f + FCHUNK])
        back = dot_nt(g[:, width:], wout[f : f + FCHUNK, :])
        act, grad = gelu_parts(pre)
        hid[:, f : f + FCHUNK] = act.astype(BF)
        dpre[:, f : f + FCHUNK] = (back * grad).astype(BF)
    res[:, :width] = dot(hid[...], wout[...]).astype(BF)
    res[:, width:] = dot_nt(dpre[...], win[...]).astype(BF)


def expert_backward_body(layer, ids, g, slope, own_in, own_out, sw_in, sw_out, res, dpre, win, wout, sem):
    waits = chosen_copies(ids[0] == layer, (own_in, own_out), (sw_in, sw_out), (win, wout), sem)
    waits[1]()
    for f in range(0, win.shape[1], FCHUNK):
        back = dot_nt(g[...], wout[f : f + FCHUNK, :])
        dpre[:, f : f + FCHUNK] = (back * slope[:, f : f + FCHUNK].astype(F32)).astype(BF)
    waits[0]()
    res[...] = dot_nt(dpre[...], win[...]).astype(BF)


def expert_grads_body(ids, *refs):
    zero, one = refs[:8], refs[8:14]
    gin, gout, g_all, h_all, d_all, p_all, sem = refs[14:]
    rows = g_all.shape[0] // 2
    width = g_all.shape[1]

    def copies(layer):
        plan = []
        for i in range(2):
            part = pl.ds(i * rows, rows)
            if layer == 0:
                srcs = zero[4 * i : 4 * i + 4]
            else:
                gd, h, p = one[3 * i : 3 * i + 3]
                srcs = (gd.at[:, pl.ds(0, width)], h, gd.at[:, pl.ds(width, width)], p)
            for k, (src, dst) in enumerate(zip(srcs, (g_all, h_all, d_all, p_all))):
                plan.append(pltpu.make_async_copy(src, dst.at[part], sem.at[4 * i + k]))
        return plan

    @pl.when(ids[0] == 0)
    def _():
        for copy in copies(0):
            copy.start()

    @pl.when(ids[0] != 0)
    def _():
        for copy in copies(1):
            copy.start()

    for copy in copies(0):
        copy.wait()
    for f in range(0, h_all.shape[1], FCHUNK):
        gout[f : f + FCHUNK, :] = dot_tn(h_all[:, f : f + FCHUNK], d_all[...])
    for f in range(0, width, FCHUNK):
        gin[f : f + FCHUNK, :] = dot_tn(g_all[:, f : f + FCHUNK], p_all[...])


VM = pltpu.VMEM
SPECS = {
    "v": pl.BlockSpec(memory_space=pltpu.VMEM),
    "s": pl.BlockSpec(memory_space=pltpu.SMEM),
    "a": pl.BlockSpec(memory_space=pl.ANY),
}


def kernel_call(name, body, outs, ins, spaces, scratch):
    return pl.pallas_call(
        body,
        out_shape=[jax.ShapeDtypeStruct(shape, dtype) for shape, dtype in outs],
        in_specs=[SPECS[c] for c in spaces],
        out_specs=[SPECS["v"] for _ in outs],
        scratch_shapes=scratch,
        name=name,
    )(*ins)


def shards(
    tokens,
    cotangent,
    routes,
    norm1_gain,
    qkv_weight,
    out_weight,
    norm2_gain,
    router_weight,
    expert_in,
    expert_out,
):
    sec = lax.axis_index("section")
    dpi = lax.axis_index("dp")
    experts = router_weight.shape[2]
    pair = lax.axis_size("dp")
    group = lax.axis_size("expert")
    micro, images, seq, width = tokens.shape
    count = images * seq
    half = width // pair
    ff = expert_in.shape[3]
    rows = -(-count // 16) * 16
    capacity = max(2, (3 * count + experts - 1) // experts)
    capacity = -(-capacity // 8) * 8
    slots = experts * pair * capacity
    ids = jnp.stack([sec, dpi]).astype(jnp.int32)
    is0 = sec == 0
    swap = [(0, 1), (1, 0)]

    def across(v):
        return lax.ppermute(v, "section", swap)

    def to_section(v, target):
        return lax.ppermute(v, "section", [(1 - target, target)])

    def along(v):
        return lax.ppermute(v, "dp", swap)

    def along_in(v, section):
        pairs = [(section * pair, section * pair + 1), (section * pair + 1, section * pair)]
        return lax.ppermute(v, ("section", "dp"), pairs)

    wq, wp = qkv_weight[0], out_weight[0]
    win, wout = expert_in[0, 0], expert_out[0, 0]
    pack = jnp.concatenate([norm1_gain, norm2_gain, router_weight[0].T], axis=0)
    pack_far = along(pack)
    pack_full = jnp.concatenate(
        [jnp.where(dpi == 0, pack, pack_far), jnp.where(dpi == 0, pack_far, pack)], axis=1
    )
    pack_other = across(pack_full)
    small = (jnp.where(is0, pack_full, pack_other), jnp.where(is0, pack_other, pack_full))
    q_far0 = along_in(wq, 0)
    p_far0 = along_in(wp, 0)
    q_near, p_near = across(wq), across(wp)
    q_sf0, p_sf0 = to_section(q_far0, 1), to_section(p_far0, 1)
    held_q, held_p, q_far0, p_far0 = lax.optimization_barrier((wq, wp, q_far0, p_far0))
    q_far1 = along_in(held_q, 1)
    p_far1 = along_in(held_p, 1)
    q_sf1, p_sf1 = to_section(q_far1, 0), to_section(p_far1, 0)
    weights = (
        (wq, q_far0, q_near, q_sf0, wp, p_far0, p_near, p_sf0),
        (wq, q_far1, q_near, q_sf1, wp, p_far1, p_near, p_sf1),
    )
    win_sw, wout_sw = across(win), across(wout)

    mine = routes[0]
    own_route = jnp.where(is0, mine[0], mine[1])
    sent_route = jnp.where(is0, mine[1], mine[0])
    got_route = across(sent_route)
    fill = ((0, rows - count), (0, 0))

    def padded_route(r):
        return jnp.pad(r.reshape(count, 2), fill, constant_values=-1)

    rc = (
        padded_route(jnp.where(is0, own_route, got_route)),
        padded_route(jnp.where(is0, got_route, own_route)),
    )
    rr = (rc[0].T, rc[1].T)
    sid = np.arange(slots)
    sid_np = np.stack([sid // (pair * capacity), sid % capacity]).astype(np.int32)
    sid_row, sid_col = jnp.asarray(sid_np), jnp.asarray(sid_np.T.copy())

    def own_micro(v):
        return jnp.pad(jnp.where(is0, v[0], v[1]).reshape(count, width), fill)

    x0 = own_micro(tokens)
    cot = own_micro(cotangent)

    wscratch = [
        pltpu.VMEM((width, 3 * width), BF),
        pltpu.VMEM((width, width), BF),
        pltpu.SemaphoreType.DMA((4,)),
    ]
    escratch = [pltpu.VMEM((width, ff), BF), pltpu.VMEM((ff, width), BF), pltpu.SemaphoreType.DMA((2,))]

    def exchange(v):
        return lax.all_to_all(v, ("expert", "dp"), split_axis=0, concat_axis=0, tiled=True)

    token_outs = [((rows, width), F32), ((rows, 3 * width), BF), ((rows, width), BF), ((rows, width), BF)]
    send, r0, qkv0, attn0, a0 = kernel_call(
        "forward_first",
        functools.partial(forward_body, 0, count, experts, False),
        [((slots, width), BF)] + token_outs,
        (ids, x0, small[0], rr[0], sid_col) + weights[0],
        "svvvv" + "a" * 8,
        wscratch,
    )
    g0 = exchange(send)
    res0, hid0, slope0 = kernel_call(
        "experts_first",
        functools.partial(expert_forward_body, 0),
        [((slots, width), BF), ((slots, ff), BF), ((slots, ff), BF)],
        (ids, g0, win, wout, win_sw, wout_sw),
        "svaaaa",
        escratch,
    )
    ret0 = exchange(res0)
    send, r1, qkv1, attn1, a1, x1 = kernel_call(
        "forward_second",
        functools.partial(forward_body, 1, count, experts, True),
        [((slots, 2 * width), BF)] + token_outs + [((rows, width), BF)],
        (ids, ret0, r0, small[0], rc[0], cot, small[1], rc[1], rr[1], sid_row, sid_col) + weights[1],
        "s" + "v" * 10 + "a" * 8,
        wscratch,
    )
    gd1 = exchange(send)
    res1, hid1, dpre1 = kernel_call(
        "experts_second",
        functools.partial(expert_both_body, 1),
        [((slots, 2 * width), BF), ((slots, ff), BF), ((slots, ff), BF)],
        (ids, gd1, win, wout, win_sw, wout_sw),
        "svaaaa",
        escratch,
    )
    ret1 = exchange(res1)
    back_outs = [((rows, 3 * width), BF), ((rows, width), BF), ((experts + 2, width), F32)]
    dq1, dr1, sm1, out1, c0, send = kernel_call(
        "backward_second",
        functools.partial(backward_body, 1, count, experts, False),
        back_outs + [((rows, width), F32), ((rows, width), BF), ((slots, width), BF)],
        (ids, ret1, cot, r1, x1, qkv1, small[1], rc[1], sid_row, r0, small[0], rc[0], rr[0], sid_col)
        + weights[1],
        "s" + "v" * 13 + "a" * 8,
        wscratch,
    )
    d0 = exchange(send)
    res0b, dpre0 = kernel_call(
        "experts_last",
        functools.partial(expert_backward_body, 0),
        [((slots, width), BF), ((slots, ff), BF)],
        (ids, d0, slope0, win, wout, win_sw, wout_sw),
        "svvaaaa",
        escratch,
    )
    ret0b = exchange(res0b)
    dq0, dr0, sm0, dh0 = kernel_call(
        "backward_first",
        functools.partial(backward_body, 0, count, experts, True),
        back_outs + [((rows, width), F32)],
        (ids, ret0, ret0b, c0, r0, x0, qkv0, small[0], rc[0], sid_row) + weights[0],
        "s" + "v" * 9 + "a" * 8,
        wscratch,
    )

    o_g0, o_hid0, o_d0, o_dpre0 = (to_section(v, 0) for v in (g0, hid0, d0, dpre0))
    o_gd1, o_hid1, o_dpre1 = (to_section(v, 1) for v in (gd1, hid1, dpre1))
    gin, gout = kernel_call(
        "expert_grads",
        expert_grads_body,
        [((width, ff), F32), ((ff, width), F32)],
        (ids, g0, hid0, d0, dpre0, o_g0, o_hid0, o_d0, o_dpre0, gd1, hid1, dpre1, o_gd1, o_hid1, o_dpre1),
        "s" + "a" * 14,
        [
            pltpu.VMEM((2 * slots, width), BF),
            pltpu.VMEM((2 * slots, ff), BF),
            pltpu.VMEM((2 * slots, width), BF),
            pltpu.VMEM((2 * slots, ff), BF),
            pltpu.SemaphoreType.DMA((8,)),
        ],
    )

    def halves(v):
        h = v.shape[1] // 2
        return v[:, :h], v[:, h:]

    def rows_side(a, attn):
        both = jnp.concatenate([a, attn], axis=1)
        pair_rows = jnp.stack([both, across(both)])
        quarter = pair_rows.reshape(2, rows, 2, pair, half)
        own = jnp.where(dpi == 0, quarter[:, :, :, 0], quarter[:, :, :, 1])
        other = jnp.where(dpi == 0, quarter[:, :, :, 1], quarter[:, :, :, 0])
        return jnp.stack([own, along(other)]).reshape(4 * rows, 2, half)

    def cols_side(dq, dr):
        (q_lo, q_hi), (r_lo, r_hi) = halves(dq), halves(dr)
        lo = jnp.concatenate([q_lo, r_lo], axis=1)
        hi = jnp.concatenate([q_hi, r_hi], axis=1)
        two = jnp.stack([jnp.where(is0, lo, hi), across(jnp.where(is0, hi, lo))])
        return jnp.stack([two, along(two)]).reshape(4 * rows, 2 * width)

    def partial_tile(a, attn, dq, dr):
        left, right = rows_side(a, attn), cols_side(dq, dr)
        split = 3 * width // 2
        return jnp.concatenate(
            [dot(left[:, 0].T, right[:, :split]), dot(left[:, 1].T, right[:, split:])], axis=1
        ).astype(BF)

    def shift(v, k):
        return lax.ppermute(v, "expert", [(i, (i + k) % group) for i in range(group)])

    me = lax.axis_index("expert")

    def reduce_all(tile):
        part = tile.shape[0] // group
        blocks = tile.reshape(group, part, tile.shape[1])
        total = lax.dynamic_index_in_dim(blocks, me, 0, keepdims=False).astype(F32)
        for k in range(1, group):
            block = lax.dynamic_index_in_dim(blocks, (me + k) % group, 0, keepdims=False)
            total = total + shift(block, k).astype(F32)
        total = total.astype(BF)
        full = jnp.zeros_like(blocks)
        full = lax.dynamic_update_index_in_dim(full, total, me, 0)
        for k in range(1, group):
            full = lax.dynamic_update_index_in_dim(full, shift(total, k), (me - k) % group, 0)
        return full.reshape(tile.shape)

    tile1 = reduce_all(partial_tile(a1, attn1, dq1, dr1))
    sm_mine = jnp.where(is0, sm0, sm1) + across(jnp.where(is0, sm1, sm0))
    sm_lo, sm_hi = halves(sm_mine)
    sm_half = jnp.where(dpi == 0, sm_lo, sm_hi) + along(jnp.where(dpi == 0, sm_hi, sm_lo))
    sm_cols = jnp.pad(sm_half.T, ((0, 0), (0, -(experts + 2) % 128))).astype(BF)
    tile0 = reduce_all(jnp.concatenate([partial_tile(a0, attn0, dq0, dr0), sm_cols], axis=1))
    small_sum = tile0[:, 2 * width :].astype(F32)
    tile0 = tile0[:, : 2 * width]
    far1, far0 = to_section(tile1, 1), to_section(tile0, 0)
    left_tile = jnp.where(is0, tile0, far1).astype(F32)
    right_tile = jnp.where(is0, far0, tile1).astype(F32)
    split = 3 * width // 2
    grad_qkv = jnp.concatenate([left_tile[:, :split], right_tile[:, :split]], axis=1)
    grad_proj = jnp.concatenate([left_tile[:, split:], right_tile[:, split:]], axis=1)

    mine_end = jnp.where(is0, dh0, out1)[:count]
    other_end = across(jnp.where(is0, out1, dh0)[:count])
    ends = jnp.stack([jnp.where(is0, mine_end, other_end), jnp.where(is0, other_end, mine_end)])
    boundary = ends.reshape(1, micro, images, seq, width)
    return (
        boundary,
        small_sum[:, 0][None],
        grad_qkv[None],
        grad_proj[None],
        small_sum[:, 1][None],
        small_sum[:, 2 : 2 + experts][None],
        gin[None, None],
        gout[None, None],
    )


def solution(mesh):
    in_specs = (
        P(None, ("expert", "dp"), None, None),
        P(None, ("expert", "dp"), None, None),
        P("section", None, ("expert", "dp"), None, None),
        P("section", "dp"),
        P("section", "dp", None),
        P("section", "dp", None),
        P("section", "dp"),
        P("section", "dp", None),
        P("section", "expert", None, "dp"),
        P("section", "expert", "dp", None),
    )
    out_specs = (
        P("section", None, ("expert", "dp"), None, None),
        P("section", "dp"),
        P("section", "dp", None),
        P("section", "dp", None),
        P("section", "dp"),
        P("section", "dp", None),
        P("section", "expert", None, "dp"),
        P("section", "expert", "dp", None),
    )
    return jax.shard_map(shards, mesh=mesh, in_specs=in_specs, out_specs=out_specs, check_vma=False)
```

time: 890 us -> 505 us (0.57)
  matrix products: 166 us -> 1.99 us
  blocking collectives: 188 us -> 43.8 us
  local copies, waits for them, and re-layouts: 131 us -> 33 us
  other arithmetic: 95.5 us -> 17.3 us
  starting transfers between devices: 49.1 us -> 125 us
  Pallas kernels: 0 us -> 71.4 us
  waiting for transfers between devices: 227 us -> 200 us
  between operations: 17.2 us -> 2.35 us
    dot_general x69 -> x4, matrix products: 166 us -> 1.99 us  [dot(): return jnp.dot(a, b, preferred_element_type=F32)]
    ppermute x4 -> x63, waiting for transfers between devices: 3.97 us -> 151 us  [the longest x28 98.5 us: shift(): lax.ppermute(v, 'expert', [(i, (i + k) % group) for i in range(group)])]
    all_to_all x6 -> x1, blocking collectives: 150 us -> 43.8 us  [exchange(): lax.all_to_all(v, ('expert', 'dp'), split_axis=0, concat_axis=0, tiled=True)]
    psum x1 -> x0, waiting for transfers between devices: 82.4 us -> none  [shards(): lax.psum(shortened(shares), 'expert')]
    ppermute x4 -> x63, starting transfers between devices: 5.14 us -> 81.4 us  [the longest x28 41.6 us: shift(): lax.ppermute(v, 'expert', [(i, (i + k) % group) for i in range(group)])]
    pallas_call x0 -> x8, Pallas kernels: none -> 71.4 us  [kernel_call(): pl.pallas_call(body, out_shape=[jax.ShapeDtypeStruct(shape, dtype) for sh...]
    all_gather x2 -> x0, waiting for transfers between devices: 54.3 us -> none  [the longest x1 36.5 us: shards(): lax.all_gather(qkv_weight, 'dp', axis=1, tiled=True)]
    reduce_sum x39 -> x0, other arithmetic: 36.4 us -> none  [the longest x6 9.75 us: owner_trip(): jnp.sum(returned.reshape(experts, pair_size, capacity, model_width), axis=1)]
  transfers between devices with their start and end apart: 16 -> 68, of which waited for: 14 -> 31; matrix products, arithmetic and copies ran while one was open for 12% -> 7% of each run, Pallas kernels for 0% -> 11%
where the time goes in v1:
time: 505 us; the launch traced here: 495 us
  waiting for transfers between devices  200 us (40%)
  starting transfers between devices  125 us (25%)
  Pallas kernels  71.4 us (14%)
  blocking collectives  43.8 us (9%)
  local copies, waits for them, and re-layouts  33 us (7%)
  other arithmetic  17.3 us (3%)
    ppermute x28, waiting for transfers between devices, shift(): lax.ppermute(v, 'expert', [(i, (i + k) % group) for i in range(group)])  98.5 us
    pallas_call x8, Pallas kernels, kernel_call(): pl.pallas_call(body, out_shape=[jax.ShapeDtypeStruct(shape, dtype) for sh...  71.4 us
    all_to_all x5, waiting for transfers between devices, exchange(): lax.all_to_all(v, ('expert', 'dp'), split_axis=0, concat_axis=0, tiled=True)  49 us
    all_to_all x5, starting transfers between devices, exchange(): lax.all_to_all(v, ('expert', 'dp'), split_axis=0, concat_axis=0, tiled=True)  44.1 us
    all_to_all x1, blocking collectives, exchange(): lax.all_to_all(v, ('expert', 'dp'), split_axis=0, concat_axis=0, tiled=True)  43.8 us
    ppermute x28, starting transfers between devices, shift(): lax.ppermute(v, 'expert', [(i, (i + k) % group) for i in range(group)])  41.6 us
    ppermute x6, waiting for transfers between devices, along(): return lax.ppermute(v, 'dp', swap)  22 us
    ppermute x13, starting transfers between devices, to_section(): return lax.ppermute(v, 'section', [(1 - target, target)])  19.6 us
  transfers between devices with their start and end apart: 68, of which 31 were waited for; matrix products, arithmetic and copies ran while one was open for 7% of the time, Pallas kernels for 11%

profile of v1, /device:TPU:28, one launch (start us, length us, event | category | flops | bytes accessed | tf_op | source)
XLA Modules:
  0.0 495.0 jit_solution(341088732032298936)
XLA Ops:
  0.6 2.4 collective-permute-start.3
  3.1 3.4 collective-permute-start.4
  8.4 17.1 %collective-permute-done.3.refs_6_.refs_11_ = bf16[384,2304]{1,0:T(8,128)(2,1)} collective-permute-done((bf16[384,2304]{1,0:T(8,128)(2,1)}, bf16[384,2304]{1,0:T(8,128)(2,1)}, u32[]{:S(2)}, u32[]{:S(2)}) %collective-permute-start.3) | collective-permute-done | bytes 1769504 | tf_op jit(solution)/shard_map/ppermute | solution.py:439
  25.5 2.5 collective-permute-start.6
  29.6 2.2 collective-permute-done
  46.4 6.6 %forward_first.1 = (bf16[512,768]{1,0:T(8,128)(2,1)}, f32[80,768]{1,0:T(8,128)}, bf16[80,2304]{1,0:T(8,128)(2,1)}, bf16[80,768]{1,0:T(8,128)(2,1)}, bf16[80,768]{1,0:T(8,128)(2,1)}) custom-call(s32[2]{0:T(128)} %pad_add_fusion.refs_0_.ids, bf16[80,768]{1,0:T(8,128)(2,1)} %pad.19.refs_1_.refs_5_, ...), custom_call_target="tpu_custom_call" | custom-call | tf_op jit(solution)/shard_map/forward_first/pallas_call | solution.py:389
  53.1 7.0 %all-to-all-start = ((bf16[16,32,768]{2,1,0:T(8,128)(2,1)}), bf16[16,32,768]{2,1,0:T(8,128)(2,1)S(1)}, u32[]{:S(2)}, u32[]{:S(2)}) async-start(bf16[16,32,768]{2,1,0:T(8,128)(2,1)} %bitcast.243), calls=%async_computation | async-start | bytes 1572864 | tf_op jit(solution)/shard_map/all_to_all | solution.py:496
  61.3 16.8 %all-to-all-done = bf16[16,32,768]{2,1,0:T(8,128)(2,1)S(1)} async-done(((bf16[16,32,768]{2,1,0:T(8,128)(2,1)}), bf16[16,32,768]{2,1,0:T(8,128)(2,1)S(1)}, u32[]{:S(2)}, u32[]{:S(2)}) %all-to-all-start) | async-done | bytes 786464 | tf_op jit(solution)/shard_map/all_to_all | solution.py:496
  79.0 7.6 %experts_first.1 = (bf16[512,768]{1,0:T(8,128)(2,1)}, bf16[512,1536]{1,0:T(8,128)(2,1)}, bf16[512,1536]{1,0:T(8,128)(2,1)}) custom-call(s32[2]{0:T(128)} %pad_add_fusion.refs_0_.ids, bf16[512,768]{1,0:T(8,128)(2,1)} %bitcast.217, bf16[768,1536]{1,0:T(8,128)(2,1)} %bitcast.200, bf16[1536,768]{1,0:T(8,128)(2,1)} %bitcast.204, ...), custom_call_target="tpu_custom_call" | custom-call | tf_op jit(solution)/shard_map/experts_first/pallas_call | solution.py:389
  86.7 7.6 %all-to-all-start.1 = ((bf16[16,32,768]{2,1,0:T(8,128)(2,1)}), bf16[16,32,768]{2,1,0:T(8,128)(2,1)S(1)}, u32[]{:S(2)}, u32[]{:S(2)}) async-start(bf16[16,32,768]{2,1,0:T(8,128)(2,1)} %bitcast.242), calls=%async_computation.1 | async-start | bytes 1572864 | tf_op jit(solution)/shard_map/all_to_all | solution.py:496
  98.6 11.8 %collective-permute-done.14.refs_18_.refs_21_ = bf16[384,768]{1,0:T(8,128)(2,1)S(1)} collective-permute-done((bf16[384,768]{1,0:T(8,128)(2,1)S(1)}, bf16[384,768]{1,0:T(8,128)(2,1)S(1)}, u32[]{:S(2)}, u32[]{:S(2)}) %collective-permute-start.14) | collective-permute-done | bytes 589856 | tf_op jit(solution)/shard_map/ppermute | solution.py:432
  112.0 8.1 %forward_second.1 = (bf16[512,1536]{1,0:T(8,128)(2,1)}, f32[80,768]{1,0:T(8,128)}, bf16[80,2304]{1,0:T(8,128)(2,1)}, bf16[80,768]{1,0:T(8,128)(2,1)}, bf16[80,768]{1,0:T(8,128)(2,1)}, /*index=5*/bf16[80,768]{1,0:T(8,128)(2,1)}) custom-call(s32[2]{0:T(128)} %pad_add_fusion.refs_0_.ids, bf16[512,768]{1,0:T(8,128)(2,1)} %bitcast.223, ...), custom_call_target="tpu_custom_call" | custom-call | tf_op jit(solution)/shard_map/forward_second/pallas_call | solution.py:389
  120.1 43.8 %all_to_all.66 = bf16[16,32,1536]{2,1,0:T(8,128)(2,1)} all-to-all(bf16[16,32,1536]{2,1,0:T(8,128)(2,1)} %bitcast.234), channel_id=1, replica_groups=mesh['section'=2,'expert'=8,'dp'=2] {'expert','dp'}, dimensions={0} | all-to-all | bytes 3145728 | tf_op jit(solution)/shard_map/all_to_all | solution.py:496
  164.0 10.1 %experts_second.1 = (bf16[512,1536]{1,0:T(8,128)(2,1)}, bf16[512,1536]{1,0:T(8,128)(2,1)}, bf16[512,1536]{1,0:T(8,128)(2,1)}) custom-call(s32[2]{0:T(128)} %pad_add_fusion.refs_0_.ids, bf16[512,1536]{1,0:T(8,128)(2,1)} %bitcast.207, bf16[768,1536]{1,0:T(8,128)(2,1)} %bitcast.201, bf16[1536,768]{1,0:T(8,128)(2,1)} %bitcast.205, ...), custom_call_target="tpu_custom_call" | custom-call | tf_op jit(solution)/shard_map/experts_second/pallas_call | solution.py:389
  174.1 7.3 %all-to-all-start.3 = ((bf16[16,32,1536]{2,1,0:T(8,128)(2,1)}), bf16[16,32,1536]{2,1,0:T(8,128)(2,1)S(1)}, u32[]{:S(2)}, u32[]{:S(2)}) async-start(bf16[16,32,1536]{2,1,0:T(8,128)(2,1)} %bitcast.233), calls=%async_computation.3 | async-start | bytes 3145728 | tf_op jit(solution)/shard_map/all_to_all | solution.py:496
  183.2 31.4 %all-to-all-done.3 = bf16[16,32,1536]{2,1,0:T(8,128)(2,1)S(1)} async-done(((bf16[16,32,1536]{2,1,0:T(8,128)(2,1)}), bf16[16,32,1536]{2,1,0:T(8,128)(2,1)S(1)}, u32[]{:S(2)}, u32[]{:S(2)}) %all-to-all-start.3) | async-done | bytes 1572896 | tf_op jit(solution)/shard_map/all_to_all | solution.py:496
  215.7 9.9 %backward_second.1 = (bf16[80,2304]{1,0:T(8,128)(2,1)}, bf16[80,768]{1,0:T(8,128)(2,1)}, f32[10,768]{1,0:T(8,128)}, f32[80,768]{1,0:T(8,128)}, bf16[80,768]{1,0:T(8,128)(2,1)}, /*index=5*/bf16[512,768]{1,0:T(8,128)(2,1)}) custom-call(s32[2]{0:T(128)} %pad_add_fusion.refs_0_.ids, bf16[512,1536]{1,0:T(8,128)(2,1)} %bitcast.225, ...), custom_call_target="tpu_custom_call" | custom-call | tf_op jit(solution)/shard_map/backward_second/pallas_call | solution.py:389
  231.6 5.1 %collective-permute-done.37 = bf16[2,80,2,384]{3,1,2,0:T(8,128)(2,1)S(1)} collective-permute-done((bf16[2,80,2,384]{3,1,2,0:T(8,128)(2,1)S(1)}, bf16[2,80,2,384]{3,1,2,0:T(8,128)(2,1)S(1)}, u32[]{:S(2)}, u32[]{:S(2)}) %collective-permute-start.37) | collective-permute-done | bytes 245792 | tf_op jit(solution)/shard_map/ppermute | solution.py:435
  237.3 8.2 %all-to-all-start.4 = ((bf16[16,32,768]{2,1,0:T(8,128)(2,1)}), bf16[16,32,768]{2,1,0:T(8,128)(2,1)S(1)}, u32[]{:S(2)}, u32[]{:S(2)}) async-start(bf16[16,32,768]{2,1,0:T(8,128)(2,1)} %bitcast.240), calls=%async_computation.4 | async-start | bytes 1572864 | tf_op jit(solution)/shard_map/all_to_all | solution.py:496
  245.6 3.3 collective-permute-done.39
  252.4 4.4 collective-permute-start.45
  258.3 4.0 collective-permute-start.42
  262.6 3.5 collective-permute-done.45
  266.2 2.8 collective-permute-done.44
  269.6 13.2 %collective-permute-done.43 = bf16[48,1536]{1,0:T(8,128)(2,1)S(1)} collective-permute-done((bf16[48,1536]{1,0:T(8,128)(2,1)S(1)}, bf16[48,1536]{1,0:T(8,128)(2,1)S(1)}, u32[]{:S(2)}, u32[]{:S(2)}) %collective-permute-start.43) | collective-permute-done | bytes 147488 | tf_op jit(solution)/shard_map/ppermute | solution.py:608
  285.9 8.6 %experts_last.1 = (bf16[512,768]{1,0:T(8,128)(2,1)}, bf16[512,1536]{1,0:T(8,128)(2,1)}) custom-call(s32[2]{0:T(128)} %pad_add_fusion.refs_0_.ids, bf16[512,768]{1,0:T(8,128)(2,1)} %bitcast.220, bf16[512,1536]{1,0:T(8,128)(2,1)} %get-tuple-element.56.slope, bf16[768,1536]{1,0:T(8,128)(2,1)} %bitcast.202, bf16[1536,768]{1,0:T(8,128)(2,1)} %bitcast.206, ...), custom_call_target="tpu_custom_call" | custom-call | tf_op jit(solution)/shard_map/experts_last/pallas_call | solution.py:389
  294.5 14.1 %all-to-all-start.5 = ((bf16[16,32,768]{2,1,0:T(8,128)(2,1)}), bf16[16,32,768]{2,1,0:T(8,128)(2,1)S(1)}, u32[]{:S(2)}, u32[]{:S(2)}) async-start(bf16[16,32,768]{2,1,0:T(8,128)(2,1)} %bitcast.241), calls=%async_computation.5 | async-start | bytes 1572864 | tf_op jit(solution)/shard_map/all_to_all | solution.py:496
  310.2 2.4 collective-permute-start.49
  316.1 9.6 %collective-permute-done.48 = bf16[48,1536]{1,0:T(8,128)(2,1)S(1)} collective-permute-done((bf16[48,1536]{1,0:T(8,128)(2,1)}, bf16[48,1536]{1,0:T(8,128)(2,1)S(1)}, u32[]{:S(2)}, u32[]{:S(2)}) %collective-permute-start.48) | collective-permute-done | bytes 147488 | tf_op jit(solution)/shard_map/ppermute | solution.py:608
  325.7 20.1 %collective-permute-done.49 = bf16[48,1536]{1,0:T(8,128)(2,1)S(1)} collective-permute-done((bf16[48,1536]{1,0:T(8,128)(2,1)}, bf16[48,1536]{1,0:T(8,128)(2,1)S(1)}, u32[]{:S(2)}, u32[]{:S(2)}) %collective-permute-start.49) | collective-permute-done | bytes 147488 | tf_op jit(solution)/shard_map/ppermute | solution.py:608
  346.7 8.7 %backward_first.1 = (bf16[80,2304]{1,0:T(8,128)(2,1)}, bf16[80,768]{1,0:T(8,128)(2,1)}, f32[10,768]{1,0:T(8,128)}, f32[80,768]{1,0:T(8,128)}) custom-call(s32[2]{0:T(128)} %pad_add_fusion.refs_0_.ids, bf16[512,768]{1,0:T(8,128)(2,1)} %bitcast.224, bf16[512,768]{1,0:T(8,128)(2,1)} %bitcast.231, bf16[80,768]{1,0:T(8,128)(2,1)} %get-tuple-element.58.refs_3_, ...), custom_call_target="tpu_custom_call" | custom-call | tf_op jit(solution)/shard_map/backward_first/pallas_call | solution.py:389
  362.3 10.6 %collective-permute-done.19 = bf16[2,80,1536]{2,1,0:T(8,128)(2,1)S(1)} collective-permute-done((bf16[2,80,1536]{2,1,0:T(8,128)(2,1)S(1)}, bf16[2,80,1536]{2,1,0:T(8,128)(2,1)S(1)}, u32[]{:S(2)}, u32[]{:S(2)}) %collective-permute-start.19) | collective-permute-done | bytes 491552 | tf_op jit(solution)/shard_map/ppermute | solution.py:435
  376.7 3.2 collective-permute-start.25
  381.4 2.4 collective-permute-start.23
  389.2 6.5 %collective-permute-done.25 = bf16[48,1664]{1,0:T(8,128)(2,1)S(1)} collective-permute-done((bf16[48,1664]{1,0:T(8,128)(2,1)S(1)}, bf16[48,1664]{1,0:T(8,128)(2,1)S(1)}, u32[]{:S(2)}, u32[]{:S(2)}) %collective-permute-start.25) | collective-permute-done | bytes 159776 | tf_op jit(solution)/shard_map/ppermute | solution.py:608
  396.9 3.2 collective-permute-done.24
  402.1 2.4 collective-permute-start.53
  404.9 2.8 collective-permute-done.53
  409.1 2.4 collective-permute-done.29
  411.4 7.9 %collective-permute-start.30 = (bf16[48,1664]{1,0:T(8,128)(2,1)S(1)}, bf16[48,1664]{1,0:T(8,128)(2,1)S(1)}, u32[]{:S(2)}, u32[]{:S(2)}) collective-permute-start(bf16[48,1664]{1,0:T(8,128)(2,1)S(1)} %get-tuple-element.107), channel_id=1, source_target_pairs={{0,4},{2,6},{4,8},{6,10},{8,12},{10,14},{12,0},{14,2},{1,5},{3,7},... | collective-permute-start | bytes 479240 | tf_op jit(solution)/shard_map/ppermute | solution.py:608
  419.3 2.8 collective-permute-done.30
  422.1 4.6 collective-permute-start.31
  426.7 5.7 %collective-permute-done.31 = bf16[48,1664]{1,0:T(8,128)(2,1)S(1)} collective-permute-done((bf16[48,1664]{1,0:T(8,128)(2,1)S(1)}, bf16[48,1664]{1,0:T(8,128)(2,1)S(1)}, u32[]{:S(2)}, u32[]{:S(2)}) %collective-permute-start.31) | collective-permute-done | bytes 159776 | tf_op jit(solution)/shard_map/ppermute | solution.py:608
  432.5 12.3 %collective-permute-done.32 = bf16[48,1664]{1,0:T(8,128)(2,1)S(1)} collective-permute-done((bf16[48,1664]{1,0:T(8,128)(2,1)S(1)}, bf16[48,1664]{1,0:T(8,128)(2,1)S(1)}, u32[]{:S(2)}, u32[]{:S(2)}) %collective-permute-start.32) | collective-permute-done | bytes 159776 | tf_op jit(solution)/shard_map/ppermute | solution.py:608
  444.9 7.9 %collective-permute-done.33 = bf16[48,1664]{1,0:T(8,128)(2,1)S(1)} collective-permute-done((bf16[48,1664]{1,0:T(8,128)(2,1)S(1)}, bf16[48,1664]{1,0:T(8,128)(2,1)S(1)}, u32[]{:S(2)}, u32[]{:S(2)}) %collective-permute-start.33) | collective-permute-done | bytes 159776 | tf_op jit(solution)/shard_map/ppermute | solution.py:608
  456.0 2.4 collective-permute-done.35
  464.5 3.4 collective-permute-start.15
  470.0 11.7 %expert_grads.1 = (f32[768,1536]{1,0:T(8,128)}, f32[1536,768]{1,0:T(8,128)}) custom-call(s32[2]{0:T(128)} %pad_add_fusion.refs_0_.ids, bf16[512,768]{1,0:T(8,128)(2,1)} %bitcast.218, bf16[512,1536]{1,0:T(8,128)(2,1)} %get-tuple-element.72.refs_1_, bf16[512,768]{1,0:T(8,128)(2,1)} %bitcast.221, bf16[512,1536]{1,0:T(8,128)(2,1)} %get-tuple-element.73.refs_3_, ...), custom_call_target="tpu_custom_call" | custom-call | tf_op jit(solution)/shard_map/expert_grads/pallas_call | solution.py:389
  (298 shorter events, 96.9 us)
Async XLA Ops:
  0.6 24.9 %collective-permute-start.3 = (bf16[384,2304]{1,0:T(8,128)(2,1)}, bf16[384,2304]{1,0:T(8,128)(2,1)}, u32[]{:S(2)}, u32[]{:S(2)}) collective-permute-start(bf16[384,2304]{1,0:T(8,128)(2,1)} %bitcast.192), channel_id=1, source_target_pairs={{0,1},{1,0},{2,3},{3,2},{4,5},{5,4},{6,7},{7,6},{8,9},{9,8},{10,11... | collective-permute-start | bytes 5308424 | tf_op jit(solution)/shard_map/ppermute | solution.py:439
  3.1 29.4 %collective-permute-start.4 = (bf16[384,768]{1,0:T(8,128)(2,1)}, bf16[384,768]{1,0:T(8,128)(2,1)S(1)}, u32[]{:S(2)}, u32[]{:S(2)}) collective-permute-start(bf16[384,768]{1,0:T(8,128)(2,1)} %bitcast.210), channel_id=1, source_target_pairs={{0,1},{1,0},{2,3},{3,2},{4,5},{5,4},{6,7},{7,6},{8,9},{9,8},{10,11... | collective-permute-start | bytes 1769480 | tf_op jit(solution)/shard_map/ppermute | solution.py:439
  6.5 38.7 %collective-permute-start.5 = (bf16[384,2304]{1,0:T(8,128)(2,1)}, bf16[384,2304]{1,0:T(8,128)(2,1)S(1)}, u32[]{:S(2)}, u32[]{:S(2)}) collective-permute-start(bf16[384,2304]{1,0:T(8,128)(2,1)} %bitcast.193), channel_id=1, source_target_pairs={{0,16},{16,0},{1,17},{17,1},{2,18},{18,2},{3,19},{19,3},{4,20},{20... | collective-permute-start | bytes 5308424 | tf_op jit(solution)/shard_map/ppermute | solution.py:429
  6.6 31.2 %collective-permute-start.7 = (bf16[384,768]{1,0:T(8,128)(2,1)}, bf16[384,768]{1,0:T(8,128)(2,1)S(1)}, u32[]{:S(2)}, u32[]{:S(2)}) collective-permute-start(bf16[384,768]{1,0:T(8,128)(2,1)} %bitcast.211), channel_id=1, source_target_pairs={{0,16},{16,0},{1,17},{17,1},{2,18},{18,2},{3,19},{19,3},{4,20},{20... | collective-permute-start | bytes 1769480 | tf_op jit(solution)/shard_map/ppermute | solution.py:429
  7.8 24.0 %collective-permute-start = (bf16[10,384]{1,0:T(8,128)(2,1)S(1)}, bf16[10,384]{1,0:T(8,128)(2,1)S(1)}, u32[]{:S(2)}, u32[]{:S(2)}) collective-permute-start(bf16[10,384]{1,0:T(8,128)(2,1)S(1)} %pad_maximum_fusion.7), channel_id=1, source_target_pairs={{0,1},{1,0},{2,3},{3,2},{4,5},{5,4},{6,7},{7,6},{8,9},{9,8},{10,11... | collective-permute-start | bytes 23048 | tf_op jit(solution)/shard_map/ppermute | solution.py:435
  25.5 19.7 %collective-permute-start.6 = (bf16[384,2304]{1,0:T(8,128)(2,1)}, bf16[384,2304]{1,0:T(8,128)(2,1)}, u32[]{:S(2)}, u32[]{:S(2)}) collective-permute-start(bf16[384,2304]{1,0:T(8,128)(2,1)} %collective-permute-done.3.refs_6_.refs_11_), channel_id=1, source_target_pairs={{0,16},{1,17},{2,18},{3,19},{4,20},{5,21},{6,22},{7,23},{8,24},{9,... | collective-permute-start | bytes 5308424 | tf_op jit(solution)/shard_map/ppermute | solution.py:432
  37.2 24.1 %collective-permute-start.9 = (bf16[768,1536]{1,0:T(8,128)(2,1)}, bf16[768,1536]{1,0:T(8,128)(2,1)}, u32[]{:S(2)}, u32[]{:S(2)}) collective-permute-start(bf16[768,1536]{1,0:T(8,128)(2,1)} %bitcast.199), channel_id=1, source_target_pairs={{0,16},{16,0},{1,17},{17,1},{2,18},{18,2},{3,19},{19,3},{4,20},{20... | collective-permute-start | bytes 7077896 | tf_op jit(solution)/shard_map/ppermute | solution.py:429
  37.8 23.5 %collective-permute-start.10 = (bf16[1536,768]{1,0:T(8,128)(2,1)}, bf16[1536,768]{1,0:T(8,128)(2,1)}, u32[]{:S(2)}, u32[]{:S(2)}) collective-permute-start(bf16[1536,768]{1,0:T(8,128)(2,1)} %bitcast.203), channel_id=1, source_target_pairs={{0,16},{16,0},{1,17},{17,1},{2,18},{18,2},{3,19},{19,3},{4,20},{20... | collective-permute-start | bytes 7077896 | tf_op jit(solution)/shard_map/ppermute | solution.py:429
  38.0 22.0 %collective-permute-start.11 = (bf16[384,2304]{1,0:T(8,128)(2,1)}, bf16[384,2304]{1,0:T(8,128)(2,1)}, u32[]{:S(2)}, u32[]{:S(2)}) collective-permute-start(bf16[384,2304]{1,0:T(8,128)(2,1)} %bitcast.194), channel_id=1, source_target_pairs={{16,17},{17,16},{18,19},{19,18},{20,21},{21,20},{22,23},{23,22},{2... | collective-permute-start | bytes 5308424 | tf_op jit(solution)/shard_map/ppermute | solution.py:439
  53.1 25.1 %all-to-all-start = ((bf16[16,32,768]{2,1,0:T(8,128)(2,1)}), bf16[16,32,768]{2,1,0:T(8,128)(2,1)S(1)}, u32[]{:S(2)}, u32[]{:S(2)}) async-start(bf16[16,32,768]{2,1,0:T(8,128)(2,1)} %bitcast.243), calls=%async_computation | async-start | bytes 1572864 | tf_op jit(solution)/shard_map/all_to_all | solution.py:496
  60.0 50.3 %collective-permute-start.12 = (bf16[384,2304]{1,0:T(8,128)(2,1)}, bf16[384,2304]{1,0:T(8,128)(2,1)}, u32[]{:S(2)}, u32[]{:S(2)}) collective-permute-start(bf16[384,2304]{1,0:T(8,128)(2,1)} %collective-permute-done.11.refs_12_.refs_15_), channel_id=1, source_target_pairs={{16,0},{17,1},{18,2},{19,3},{20,4},{21,5},{22,6},{23,7},{24,8},{25... | collective-permute-start | bytes 5308424 | tf_op jit(solution)/shard_map/ppermute | solution.py:432
  86.7 24.5 %all-to-all-start.1 = ((bf16[16,32,768]{2,1,0:T(8,128)(2,1)}), bf16[16,32,768]{2,1,0:T(8,128)(2,1)S(1)}, u32[]{:S(2)}, u32[]{:S(2)}) async-start(bf16[16,32,768]{2,1,0:T(8,128)(2,1)} %bitcast.242), calls=%async_computation.1 | async-start | bytes 1572864 | tf_op jit(solution)/shard_map/all_to_all | solution.py:496
  95.0 15.3 %collective-permute-start.14 = (bf16[384,768]{1,0:T(8,128)(2,1)S(1)}, bf16[384,768]{1,0:T(8,128)(2,1)S(1)}, u32[]{:S(2)}, u32[]{:S(2)}) collective-permute-start(bf16[384,768]{1,0:T(8,128)(2,1)S(1)} %collective-permute-done.13.refs_16_.refs_19_), channel_id=1, source_target_pairs={{16,0},{17,1},{18,2},{19,3},{20,4},{21,5},{22,6},{23,7},{24,8},{25... | collective-permute-start | bytes 1769480 | tf_op jit(solution)/shard_map/ppermute | solution.py:432
  174.1 40.4 %all-to-all-start.3 = ((bf16[16,32,1536]{2,1,0:T(8,128)(2,1)}), bf16[16,32,1536]{2,1,0:T(8,128)(2,1)S(1)}, u32[]{:S(2)}, u32[]{:S(2)}) async-start(bf16[16,32,1536]{2,1,0:T(8,128)(2,1)} %bitcast.233), calls=%async_computation.3 | async-start | bytes 3145728 | tf_op jit(solution)/shard_map/all_to_all | solution.py:496
  181.7 49.9 %collective-permute-start.16 = (bf16[80,1536]{1,0:T(8,128)(2,1)S(1)}, bf16[80,1536]{1,0:T(8,128)(2,1)S(1)}, u32[]{:S(2)}, u32[]{:S(2)}) collective-permute-start(bf16[80,1536]{1,0:T(8,128)(2,1)S(1)} %constant_dynamic-update-slice_fusion), channel_id=1, source_target_pairs={{0,16},{16,0},{1,17},{17,1},{2,18},{18,2},{3,19},{19,3},{4,20},{20... | collective-permute-start | bytes 737288 | tf_op jit(solution)/shard_map/ppermute | solution.py:429
  230.2 18.7 %collective-permute-start.39 = (bf16[2,80,1536]{2,1,0:T(8,128)(2,1)}, bf16[2,80,1536]{2,1,0:T(8,128)(2,1)}, u32[]{:S(2)}, u32[]{:S(2)}) collective-permute-start(bf16[2,80,1536]{2,1,0:T(8,128)(2,1)} %get-tuple-element.128), channel_id=1, source_target_pairs={{0,1},{1,0},{2,3},{3,2},{4,5},{5,4},{6,7},{7,6},{8,9},{9,8},{10,11... | collective-permute-start | bytes 1474568 | tf_op jit(solution)/shard_map/ppermute | solution.py:435
  237.3 47.7 %all-to-all-start.4 = ((bf16[16,32,768]{2,1,0:T(8,128)(2,1)}), bf16[16,32,768]{2,1,0:T(8,128)(2,1)S(1)}, u32[]{:S(2)}, u32[]{:S(2)}) async-start(bf16[16,32,768]{2,1,0:T(8,128)(2,1)} %bitcast.240), calls=%async_computation.4 | async-start | bytes 1572864 | tf_op jit(solution)/shard_map/all_to_all | solution.py:496
  251.0 11.6 %collective-permute-start.46 = (bf16[48,1536]{1,0:T(8,128)(2,1)S(1)}, bf16[48,1536]{1,0:T(8,128)(2,1)S(1)}, u32[]{:S(2)}, u32[]{:S(2)}) collective-permute-start(bf16[48,1536]{1,0:T(8,128)(2,1)S(1)} %fusion.32), channel_id=1, source_target_pairs={{0,14},{2,0},{4,2},{6,4},{8,6},{10,8},{12,10},{14,12},{1,15},{3,1}... | collective-permute-start | bytes 442376 | tf_op jit(solution)/shard_map/ppermute | solution.py:608
  252.4 13.7 %collective-permute-start.45 = (bf16[48,1536]{1,0:T(8,128)(2,1)S(1)}, bf16[48,1536]{1,0:T(8,128)(2,1)S(1)}, u32[]{:S(2)}, u32[]{:S(2)}) collective-permute-start(bf16[48,1536]{1,0:T(8,128)(2,1)S(1)} %get-tuple-element.122), channel_id=1, source_target_pairs={{0,12},{2,14},{4,0},{6,2},{8,4},{10,6},{12,8},{14,10},{1,13},{3,15... | collective-permute-start | bytes 442376 | tf_op jit(solution)/shard_map/ppermute | solution.py:608
  256.9 12.1 %collective-permute-start.44 = (bf16[48,1536]{1,0:T(8,128)(2,1)S(1)}, bf16[48,1536]{1,0:T(8,128)(2,1)S(1)}, u32[]{:S(2)}, u32[]{:S(2)}) collective-permute-start(bf16[48,1536]{1,0:T(8,128)(2,1)S(1)} %get-tuple-element.121), channel_id=1, source_target_pairs={{0,10},{2,12},{4,14},{6,0},{8,2},{10,4},{12,6},{14,8},{1,11},{3,13... | collective-permute-start | bytes 442376 | tf_op jit(solution)/shard_map/ppermute | solution.py:608
  257.0 25.8 %collective-permute-start.43 = (bf16[48,1536]{1,0:T(8,128)(2,1)S(1)}, bf16[48,1536]{1,0:T(8,128)(2,1)S(1)}, u32[]{:S(2)}, u32[]{:S(2)}) collective-permute-start(bf16[48,1536]{1,0:T(8,128)(2,1)S(1)} %get-tuple-element.120), channel_id=1, source_target_pairs={{0,8},{2,10},{4,12},{6,14},{8,0},{10,2},{12,4},{14,6},{1,9},{3,11}... | collective-permute-start | bytes 442376 | tf_op jit(solution)/shard_map/ppermute | solution.py:608
  258.3 24.8 %collective-permute-start.42 = (bf16[48,1536]{1,0:T(8,128)(2,1)S(1)}, bf16[48,1536]{1,0:T(8,128)(2,1)S(1)}, u32[]{:S(2)}, u32[]{:S(2)}) collective-permute-start(bf16[48,1536]{1,0:T(8,128)(2,1)S(1)} %get-tuple-element.119), channel_id=1, source_target_pairs={{0,6},{2,8},{4,10},{6,12},{8,14},{10,0},{12,2},{14,4},{1,7},{3,9},... | collective-permute-start | bytes 442376 | tf_op jit(solution)/shard_map/ppermute | solution.py:608
  262.6 20.6 %collective-permute-start.41 = (bf16[48,1536]{1,0:T(8,128)(2,1)S(1)}, bf16[48,1536]{1,0:T(8,128)(2,1)S(1)}, u32[]{:S(2)}, u32[]{:S(2)}) collective-permute-start(bf16[48,1536]{1,0:T(8,128)(2,1)S(1)} %get-tuple-element.118), channel_id=1, source_target_pairs={{0,4},{2,6},{4,8},{6,10},{8,12},{10,14},{12,0},{14,2},{1,5},{3,7},... | collective-permute-start | bytes 442376 | tf_op jit(solution)/shard_map/ppermute | solution.py:608
  266.1 17.9 %collective-permute-start.40 = (bf16[48,1536]{1,0:T(8,128)(2,1)S(1)}, bf16[48,1536]{1,0:T(8,128)(2,1)S(1)}, u32[]{:S(2)}, u32[]{:S(2)}) collective-permute-start(bf16[48,1536]{1,0:T(8,128)(2,1)S(1)} %get-tuple-element.117), channel_id=1, source_target_pairs={{0,2},{2,4},{4,6},{6,8},{8,10},{10,12},{12,14},{14,0},{1,3},{3,5},... | collective-permute-start | bytes 442376 | tf_op jit(solution)/shard_map/ppermute | solution.py:608
  269.0 39.5 %collective-permute-start.17 = (bf16[2,80,2,384]{3,1,2,0:T(8,128)(2,1)S(1)}, bf16[2,80,2,384]{3,1,2,0:T(8,128)(2,1)}, u32[]{:S(2)}, u32[]{:S(2)}) collective-permute-start(bf16[2,80,2,384]{3,1,2,0:T(8,128)(2,1)S(1)} %get-tuple-element.132), channel_id=1, source_target_pairs={{0,1},{1,0},{2,3},{3,2},{4,5},{5,4},{6,7},{7,6},{8,9},{9,8},{10,11... | collective-permute-start | bytes 737288 | tf_op jit(solution)/shard_map/ppermute | solution.py:435
  285.0 30.5 %collective-permute-start.47 = (bf16[48,1536]{1,0:T(8,128)(2,1)}, bf16[48,1536]{1,0:T(8,128)(2,1)S(1)}, u32[]{:S(2)}, u32[]{:S(2)}) collective-permute-start(bf16[48,1536]{1,0:T(8,128)(2,1)} %get-tuple-element.105), channel_id=1, source_target_pairs={{0,2},{2,4},{4,6},{6,8},{8,10},{10,12},{12,14},{14,0},{1,3},{3,5},... | collective-permute-start | bytes 442376 | tf_op jit(solution)/shard_map/ppermute | solution.py:608
  294.5 51.4 %all-to-all-start.5 = ((bf16[16,32,768]{2,1,0:T(8,128)(2,1)}), bf16[16,32,768]{2,1,0:T(8,128)(2,1)S(1)}, u32[]{:S(2)}, u32[]{:S(2)}) async-start(bf16[16,32,768]{2,1,0:T(8,128)(2,1)} %bitcast.241), calls=%async_computation.5 | async-start | bytes 1572864 | tf_op jit(solution)/shard_map/all_to_all | solution.py:496
  309.6 16.1 %collective-permute-start.48 = (bf16[48,1536]{1,0:T(8,128)(2,1)}, bf16[48,1536]{1,0:T(8,128)(2,1)S(1)}, u32[]{:S(2)}, u32[]{:S(2)}) collective-permute-start(bf16[48,1536]{1,0:T(8,128)(2,1)} %get-tuple-element.105), channel_id=1, source_target_pairs={{0,4},{2,6},{4,8},{6,10},{8,12},{10,14},{12,0},{14,2},{1,5},{3,7},... | collective-permute-start | bytes 442376 | tf_op jit(solution)/shard_map/ppermute | solution.py:608
  310.2 35.6 %collective-permute-start.49 = (bf16[48,1536]{1,0:T(8,128)(2,1)}, bf16[48,1536]{1,0:T(8,128)(2,1)S(1)}, u32[]{:S(2)}, u32[]{:S(2)}) collective-permute-start(bf16[48,1536]{1,0:T(8,128)(2,1)} %get-tuple-element.105), channel_id=1, source_target_pairs={{0,6},{2,8},{4,10},{6,12},{8,14},{10,0},{12,2},{14,4},{1,7},{3,9},... | collective-permute-start | bytes 442376 | tf_op jit(solution)/shard_map/ppermute | solution.py:608
  312.6 47.9 %collective-permute-start.50 = (bf16[48,1536]{1,0:T(8,128)(2,1)}, bf16[48,1536]{1,0:T(8,128)(2,1)}, u32[]{:S(2)}, u32[]{:S(2)}) collective-permute-start(bf16[48,1536]{1,0:T(8,128)(2,1)} %get-tuple-element.105), channel_id=1, source_target_pairs={{0,8},{2,10},{4,12},{6,14},{8,0},{10,2},{12,4},{14,6},{1,9},{3,11}... | collective-permute-start | bytes 442376 | tf_op jit(solution)/shard_map/ppermute | solution.py:608
  314.1 60.6 %collective-permute-start.51 = (bf16[48,1536]{1,0:T(8,128)(2,1)}, bf16[48,1536]{1,0:T(8,128)(2,1)}, u32[]{:S(2)}, u32[]{:S(2)}) collective-permute-start(bf16[48,1536]{1,0:T(8,128)(2,1)} %get-tuple-element.105), channel_id=1, source_target_pairs={{0,10},{2,12},{4,14},{6,0},{8,2},{10,4},{12,6},{14,8},{1,11},{3,13... | collective-permute-start | bytes 442376 | tf_op jit(solution)/shard_map/ppermute | solution.py:608
  315.5 64.4 %collective-permute-start.52 = (bf16[48,1536]{1,0:T(8,128)(2,1)}, bf16[48,1536]{1,0:T(8,128)(2,1)}, u32[]{:S(2)}, u32[]{:S(2)}) collective-permute-start(bf16[48,1536]{1,0:T(8,128)(2,1)} %get-tuple-element.105), channel_id=1, source_target_pairs={{0,12},{2,14},{4,0},{6,2},{8,4},{10,6},{12,8},{14,10},{1,13},{3,15... | collective-permute-start | bytes 442376 | tf_op jit(solution)/shard_map/ppermute | solution.py:608
  359.4 13.6 %collective-permute-start.19 = (bf16[2,80,1536]{2,1,0:T(8,128)(2,1)S(1)}, bf16[2,80,1536]{2,1,0:T(8,128)(2,1)S(1)}, u32[]{:S(2)}, u32[]{:S(2)}) collective-permute-start(bf16[2,80,1536]{2,1,0:T(8,128)(2,1)S(1)} %get-tuple-element.134), channel_id=1, source_target_pairs={{0,1},{1,0},{2,3},{3,2},{4,5},{5,4},{6,7},{7,6},{8,9},{9,8},{10,11... | collective-permute-start | bytes 1474568 | tf_op jit(solution)/shard_map/ppermute | solution.py:435
  376.7 11.2 %collective-permute-start.26 = (bf16[48,1664]{1,0:T(8,128)(2,1)S(1)}, bf16[48,1664]{1,0:T(8,128)(2,1)S(1)}, u32[]{:S(2)}, u32[]{:S(2)}) collective-permute-start(bf16[48,1664]{1,0:T(8,128)(2,1)S(1)} %get-tuple-element.113), channel_id=1, source_target_pairs={{0,10},{2,12},{4,14},{6,0},{8,2},{10,4},{12,6},{14,8},{1,11},{3,13... | collective-permute-start | bytes 479240 | tf_op jit(solution)/shard_map/ppermute | solution.py:608
  376.7 18.9 %collective-permute-start.25 = (bf16[48,1664]{1,0:T(8,128)(2,1)S(1)}, bf16[48,1664]{1,0:T(8,128)(2,1)S(1)}, u32[]{:S(2)}, u32[]{:S(2)}) collective-permute-start(bf16[48,1664]{1,0:T(8,128)(2,1)S(1)} %get-tuple-element.114), channel_id=1, source_target_pairs={{0,8},{2,10},{4,12},{6,14},{8,0},{10,2},{12,4},{14,6},{1,9},{3,11}... | collective-permute-start | bytes 479240 | tf_op jit(solution)/shard_map/ppermute | solution.py:608
  379.9 20.2 %collective-permute-start.24 = (bf16[48,1664]{1,0:T(8,128)(2,1)S(1)}, bf16[48,1664]{1,0:T(8,128)(2,1)S(1)}, u32[]{:S(2)}, u32[]{:S(2)}) collective-permute-start(bf16[48,1664]{1,0:T(8,128)(2,1)S(1)} %get-tuple-element.115), channel_id=1, source_target_pairs={{0,6},{2,8},{4,10},{6,12},{8,14},{10,0},{12,2},{14,4},{1,7},{3,9},... | collective-permute-start | bytes 479240 | tf_op jit(solution)/shard_map/ppermute | solution.py:608
  381.4 20.6 %collective-permute-start.23 = (bf16[48,1664]{1,0:T(8,128)(2,1)S(1)}, bf16[48,1664]{1,0:T(8,128)(2,1)S(1)}, u32[]{:S(2)}, u32[]{:S(2)}) collective-permute-start(bf16[48,1664]{1,0:T(8,128)(2,1)S(1)} %get-tuple-element.116), channel_id=1, source_target_pairs={{0,4},{2,6},{4,8},{6,10},{8,12},{10,14},{12,0},{14,2},{1,5},{3,7},... | collective-permute-start | bytes 479240 | tf_op jit(solution)/shard_map/ppermute | solution.py:608
  383.8 20.6 %collective-permute-start.22 = (bf16[48,1664]{1,0:T(8,128)(2,1)S(1)}, bf16[48,1664]{1,0:T(8,128)(2,1)S(1)}, u32[]{:S(2)}, u32[]{:S(2)}) collective-permute-start(bf16[48,1664]{1,0:T(8,128)(2,1)S(1)} %get-tuple-element.110), channel_id=1, source_target_pairs={{0,2},{2,4},{4,6},{6,8},{8,10},{10,12},{12,14},{14,0},{1,3},{3,5},... | collective-permute-start | bytes 479240 | tf_op jit(solution)/shard_map/ppermute | solution.py:608
  387.9 56.9 %collective-permute-start.56 = (bf16[512,768]{1,0:T(8,128)(2,1)S(1)}, bf16[512,768]{1,0:T(8,128)(2,1)S(1)}, u32[]{:S(2)}, u32[]{:S(2)}) collective-permute-start(bf16[512,768]{1,0:T(8,128)(2,1)S(1)} %bitcast.219), channel_id=1, source_target_pairs={{16,0},{17,1},{18,2},{19,3},{20,4},{21,5},{22,6},{23,7},{24,8},{25... | collective-permute-start | bytes 2359304 | tf_op jit(solution)/shard_map/ppermute | solution.py:432
  395.7 57.4 %collective-permute-start.57 = (bf16[512,1536]{1,0:T(8,128)(2,1)S(1)}, bf16[512,1536]{1,0:T(8,128)(2,1)S(1)}, u32[]{:S(2)}, u32[]{:S(2)}) collective-permute-start(bf16[512,1536]{1,0:T(8,128)(2,1)S(1)} %copy-done.22), channel_id=1, source_target_pairs={{16,0},{17,1},{18,2},{19,3},{20,4},{21,5},{22,6},{23,7},{24,8},{25... | collective-permute-start | bytes 4718600 | tf_op jit(solution)/shard_map/ppermute | solution.py:432
  400.2 62.9 %collective-permute-start.60 = (bf16[512,1536]{1,0:T(8,128)(2,1)S(1)}, bf16[512,1536]{1,0:T(8,128)(2,1)S(1)}, u32[]{:S(2)}, u32[]{:S(2)}) collective-permute-start(bf16[512,1536]{1,0:T(8,128)(2,1)S(1)} %bitcast.209), channel_id=1, source_target_pairs={{0,16},{1,17},{2,18},{3,19},{4,20},{5,21},{6,22},{7,23},{8,24},{9,... | collective-permute-start | bytes 4718600 | tf_op jit(solution)/shard_map/ppermute | solution.py:432
  407.7 52.0 %collective-permute-start.54 = (bf16[384,1536]{1,0:T(8,128)(2,1)S(1)}, bf16[384,1536]{1,0:T(8,128)(2,1)S(1)}, u32[]{:S(2)}, u32[]{:S(2)}) collective-permute-start(bf16[384,1536]{1,0:T(8,128)(2,1)S(1)} %bitcast.230), channel_id=1, source_target_pairs={{0,16},{1,17},{2,18},{3,19},{4,20},{5,21},{6,22},{7,23},{8,24},{9,... | collective-permute-start | bytes 3538952 | tf_op jit(solution)/shard_map/ppermute | solution.py:432
  432.5 12.3 %collective-permute-start.32 = (bf16[48,1664]{1,0:T(8,128)(2,1)S(1)}, bf16[48,1664]{1,0:T(8,128)(2,1)S(1)}, u32[]{:S(2)}, u32[]{:S(2)}) collective-permute-start(bf16[48,1664]{1,0:T(8,128)(2,1)S(1)} %get-tuple-element.107), channel_id=1, source_target_pairs={{0,8},{2,10},{4,12},{6,14},{8,0},{10,2},{12,4},{14,6},{1,9},{3,11}... | collective-permute-start | bytes 479240 | tf_op jit(solution)/shard_map/ppermute | solution.py:608
  453.1 11.3 %collective-permute-start.61 = (bf16[512,1536]{1,0:T(8,128)(2,1)S(1)}, bf16[512,1536]{1,0:T(8,128)(2,1)S(1)}, u32[]{:S(2)}, u32[]{:S(2)}) collective-permute-start(bf16[512,1536]{1,0:T(8,128)(2,1)S(1)} %copy-done.23), channel_id=1, source_target_pairs={{0,16},{1,17},{2,18},{3,19},{4,20},{5,21},{6,22},{7,23},{8,24},{9,... | collective-permute-start | bytes 4718600 | tf_op jit(solution)/shard_map/ppermute | solution.py:432
  454.6 13.3 %collective-permute-start.62 = (bf16[512,1536]{1,0:T(8,128)(2,1)S(1)}, bf16[512,1536]{1,0:T(8,128)(2,1)S(1)}, u32[]{:S(2)}, u32[]{:S(2)}) collective-permute-start(bf16[512,1536]{1,0:T(8,128)(2,1)S(1)} %copy-done.24), channel_id=1, source_target_pairs={{0,16},{1,17},{2,18},{3,19},{4,20},{5,21},{6,22},{7,23},{8,24},{9,... | collective-permute-start | bytes 4718600 | tf_op jit(solution)/shard_map/ppermute | solution.py:432
  458.3 11.6 %collective-permute-start.59 = (bf16[512,1536]{1,0:T(8,128)(2,1)S(1)}, bf16[512,1536]{1,0:T(8,128)(2,1)}, u32[]{:S(2)}, u32[]{:S(2)}) collective-permute-start(bf16[512,1536]{1,0:T(8,128)(2,1)S(1)} %copy-done.25), channel_id=1, source_target_pairs={{16,0},{17,1},{18,2},{19,3},{20,4},{21,5},{22,6},{23,7},{24,8},{25... | collective-permute-start | bytes 4718600 | tf_op jit(solution)/shard_map/ppermute | solution.py:432
  463.1 25.5 %collective-permute-start.55 = (bf16[384,1536]{1,0:T(8,128)(2,1)}, bf16[384,1536]{1,0:T(8,128)(2,1)}, u32[]{:S(2)}, u32[]{:S(2)}) collective-permute-start(bf16[384,1536]{1,0:T(8,128)(2,1)} %get-tuple-element.109), channel_id=1, source_target_pairs={{16,0},{17,1},{18,2},{19,3},{20,4},{21,5},{22,6},{23,7},{24,8},{25... | collective-permute-start | bytes 3538952 | tf_op jit(solution)/shard_map/ppermute | solution.py:432
  464.5 17.3 %collective-permute-start.15 = (f32[65,768]{1,0:T(8,128)S(1)}, f32[65,768]{1,0:T(8,128)S(1)}, u32[]{:S(2)}, u32[]{:S(2)}) collective-permute-start(f32[65,768]{1,0:T(8,128)S(1)} %slice_select_fusion), channel_id=1, source_target_pairs={{0,16},{16,0},{1,17},{17,1},{2,18},{18,2},{3,19},{19,3},{4,20},{20... | collective-permute-start | bytes 599048 | tf_op jit(solution)/shard_map/ppermute | solution.py:429
  (70 other events, 673.0 us)
